TPU v7x, 256 devices: a whole 4x4x8 slice. The times are simulated.
256 devices in a mesh: walker: 16 (over z, core), col: 16 (over y, x).
Axes of the slice: x: 4, y: 4, z: 8, core: 2. Of those that a mesh axis runs over, the one named last changes fastest.
Arguments:
- inverses: float32 [16, 4096, 4096], P('walker', None, 'col'), may hold values from -0.2 to 2.2
- table: bfloat16 [512, 64, 4096], P('walker', None, 'col'), may hold values from -0.23925781 to 0.23925781
- spots: float32 [3, 6, 16, 64], P(None, None, 'walker'), may hold values from 0 to 1
- groups: int32 [6, 16, 64, 1], P(None, 'walker'), may hold values from 0 to 15; in each aligned block of 64 rows (0 to 63, 64 to 127, ..., all dimensions but the last counted through in order) at most 8 rows name the same one
- bricks: int32 [6, 16, 64], P(None, 'walker'), may hold values from 0 to 31
- accept: int32 [6, 16, 64], P(None, 'walker'), may hold values 0 or 1
- movers: int32 [6, 16, 64], P(None, 'walker'), may hold values from 0 to 4095, as said below
- old_rows: bfloat16 [6, 16, 64, 4096], P(None, 'walker', None, 'col'), may hold values from -0.079589844 to 0.079589844
Outputs:
- updated: float32 [16, 4096, 4096], P('walker', None, 'col')
Inputs may be any that keep to these rules, and one draw needn't show every extreme that they name: `groups`: in each window, at most 8 of one walker's 64 moves name one server group, and in some windows and walkers exactly 8 do. `movers`: the 64 electrons of one window and walker are distinct.
All inputs are finite; a program needn't handle non-finite values. No bound on the sum of `accept` on one device may be relied on, other than what follows from the above.
Results may differ from a plain program's by a relative error of at most 0.005.
Values may be sent and summed in bfloat16 or wider, within the bound.
No kernel may reach another device: no remote copies, remote signals or barrier semaphores. Data moves between devices by JAX's collectives and lax.ppermute only.
A program may use at most 128 MiB of HBM per device.

v0:
```python
import jax
import jax.numpy as jnp
from jax import lax
from jax.experimental import pallas as pl
from jax.experimental.pallas import tpu as pltpu
from jax.sharding import PartitionSpec as P

N = 4096
K = 64
ROUNDS = 6
CAP = 8
SERVERS = 16
COLS = 16
BLOCK = N // COLS
ALL = ROUNDS * K
SIDE = 4
SHARE = 48
SLOTS = ROUNDS * CAP
HIGHEST = lax.Precision.HIGHEST
NT = (((1,), (1,)), ((), ()))
bf16 = jnp.bfloat16
f32 = jnp.float32
VMEM = pl.BlockSpec(memory_space=pltpu.VMEM)
ANY = pl.BlockSpec(memory_space=pl.ANY)
SMEM = pl.BlockSpec(memory_space=pltpu.SMEM)


def iota(shape, dim):
    return lax.broadcasted_iota(jnp.int32, shape, dim)


def to_column(row):
    count = row.shape[1]
    square = jnp.broadcast_to(row, (count, count))
    same = iota((count, count), 0) == iota((count, count), 1)
    return jnp.sum(jnp.where(same, square, 0), axis=1, keepdims=True)


def plan_kernel(
    groups_ref, bricks_ref, accept_ref, movers_ref, spots_ref,
    send_ref, target_ref, movers_row_ref, key_ref,
):
    total = jnp.zeros((SERVERS * CAP, 128), f32)
    earlier = iota((K, K), 0) < iota((K, K), 1)
    mover_cols = []
    for window in range(ROUNDS):
        server_row = groups_ref[window]
        server_col = to_column(server_row)
        same = jnp.broadcast_to(server_row, (K, K)) == jnp.broadcast_to(server_col, (K, K))
        order_row = jnp.sum(jnp.where(same & earlier, 1, 0), axis=0, keepdims=True)
        place_row = server_row * CAP + order_row
        placed = jnp.where(
            iota((SERVERS * CAP, K), 0) == jnp.broadcast_to(place_row, (SERVERS * CAP, K)), 1.0, 0.0
        ).astype(f32)
        field = iota((8, K), 0)
        rows = jnp.where(field == 0, spots_ref[0, window], 0.0)
        rows = jnp.where(field == 1, spots_ref[1, window], rows)
        rows = jnp.where(field == 2, spots_ref[2, window], rows)
        rows = jnp.where(field == 3, (bricks_ref[window] + 1).astype(f32), rows)
        parts = []
        if window:
            parts.append(jnp.zeros((8 * window, K), f32))
        parts.append(rows)
        parts.append(jnp.zeros((120 - 8 * window, K), f32))
        total = total + lax.dot_general(
            placed, jnp.concatenate(parts, axis=0), NT, precision=HIGHEST,
            preferred_element_type=f32,
        )
        answer_row = server_row * SLOTS + window * CAP + order_row
        code = to_column(answer_row * 2 + accept_ref[window])
        target_ref[window * K : (window + 1) * K, :] = jnp.broadcast_to(code, (K, 128))
        movers_row_ref[:, window * K : (window + 1) * K] = movers_ref[window]
        mover_cols.append(to_column(movers_ref[window]))
    owner_row = movers_row_ref[...] // BLOCK
    owner_col = jnp.concatenate(mover_cols, axis=0) // BLOCK
    same = jnp.broadcast_to(owner_row, (ALL, ALL)) == jnp.broadcast_to(owner_col, (ALL, ALL))
    before = iota((ALL, ALL), 1) < iota((ALL, ALL), 0)
    rank_col = jnp.sum(jnp.where(same & before, 1, 0), axis=1, keepdims=True)
    key_ref[...] = jnp.broadcast_to(owner_col * ALL + rank_col, (ALL, 128))
    turns = jnp.max(rank_col, axis=0, keepdims=True) // SHARE + 1
    lane = iota((SERVERS * CAP, 128), 1)
    turns = jnp.broadcast_to(turns, (SERVERS * CAP, 128)).astype(f32)
    send_ref[...] = jnp.where(lane == 127, turns, total)


def basis_at(fraction, which):
    remain = 1.0 - fraction
    square = fraction * fraction
    cubed = square * fraction
    first = remain * remain * remain / 6.0
    second = (3.0 * cubed - 6.0 * square + 4.0) / 6.0
    third = (-3.0 * cubed + 3.0 * square + 3.0 * fraction + 1.0) / 6.0
    fourth = cubed / 6.0
    return jnp.where(
        which == 0, first, jnp.where(which == 1, second, jnp.where(which == 2, third, fourth))
    )


def serve_kernel(got_ref, table_ref, out_ref, turns_ref):
    turns_ref[0] = jnp.max(got_ref[:, 127:128]).astype(jnp.int32)
    rows = SERVERS * CAP
    point = iota((rows, 128), 1) % 64
    answers = []
    for window in range(ROUNDS):
        def column(field):
            at = 8 * window + field
            return jnp.broadcast_to(got_ref[:, at : at + 1], (rows, 128))
        weight = (
            basis_at(column(0), point // 16)
            * basis_at(column(1), (point // 4) % 4)
            * basis_at(column(2), point % 4)
        )
        brick = column(3).astype(jnp.int32) - 1
        half = iota((rows, 128), 1) // 64
        spread = jnp.concatenate(
            [jnp.where(brick == 2 * pair + half, weight, 0.0).astype(bf16) for pair in range(16)],
            axis=1,
        )
        answer = jnp.dot(spread, table_ref[...], preferred_element_type=f32)
        answers.append(answer.reshape(SERVERS, CAP, BLOCK))
        if window % 2:
            out_ref[:, (window - 1) * CAP : (window + 1) * CAP, :] = jnp.concatenate(
                answers[-2:], axis=1
            ).astype(bf16)


def collect_kernel(target_ref, answers_ref, old_ref, out_ref):
    code = target_ref[...]
    target = code // 2
    onehot = jnp.concatenate(
        [
            jnp.where(target == piece * 128 + iota((ALL, 128), 1), 1.0, 0.0).astype(bf16)
            for piece in range(SERVERS * SLOTS // 128)
        ],
        axis=1,
    )
    values = jnp.dot(onehot, answers_ref[...], preferred_element_type=f32)
    accepted = jnp.concatenate([code % 2, code % 2], axis=1).astype(f32)
    values = values.astype(bf16).astype(f32)
    out_ref[...] = (accepted * (values - old_ref[...].astype(f32))).astype(bf16)


def pick_kernel(turn_ref, movers_ref, key_ref, inverse_ref, out_ref, chosen):
    @pl.when(pl.program_id(0) == 0)
    def _():
        local_row = movers_ref[...] - lax.axis_index("col") * BLOCK
        placed = jnp.where(
            jnp.broadcast_to(local_row, (BLOCK, ALL)) == iota((BLOCK, ALL), 0), 1.0, 0.0
        ).astype(bf16)
        rank = key_ref[...] % ALL - turn_ref[0] * SHARE
        ranked = jnp.where(rank == iota((ALL, 128), 1), 1.0, 0.0).astype(bf16)
        picks = jnp.dot(placed, ranked, preferred_element_type=f32)
        chosen[...] = picks.T[:SHARE].astype(bf16)

    picked = lax.dot_general(
        chosen[...], inverse_ref[...].astype(bf16), NT, preferred_element_type=f32
    ).astype(bf16)
    for piece in range(out_ref.shape[0]):
        out_ref[piece] = picked[:, piece * BLOCK : (piece + 1) * BLOCK]


def place_kernel(turn_ref, key_ref, got_ref, out_ref):
    key = key_ref[...]
    rank = key % ALL - turn_ref[0] * SHARE
    spot = jnp.where((rank >= 0) & (rank < SHARE), (key // ALL) * SHARE + rank, -1)
    onehot = jnp.concatenate(
        [
            jnp.where(spot == piece * 128 + iota((ALL, 128), 1), 1.0, 0.0).astype(bf16)
            for piece in range(COLS * SHARE // 128)
        ],
        axis=1,
    )
    out_ref[...] = jnp.dot(onehot, got_ref[...], preferred_element_type=f32).T.astype(bf16)


def pick(turn, movers_row, key, inverse):
    step = 4
    return pl.pallas_call(
        pick_kernel,
        grid=(COLS // step,),
        in_specs=[
            SMEM,
            pl.BlockSpec((1, ALL), lambda i: (0, 0)),
            pl.BlockSpec((ALL, 128), lambda i: (0, 0)),
            pl.BlockSpec((step * BLOCK, BLOCK), lambda i: (i, 0)),
        ],
        out_specs=pl.BlockSpec((step, SHARE, BLOCK), lambda i: (i, 0, 0)),
        out_shape=jax.ShapeDtypeStruct((COLS, SHARE, BLOCK), bf16),
        scratch_shapes=[pltpu.VMEM((SHARE, BLOCK), bf16)],
        compiler_params=pltpu.CompilerParams(vmem_limit_bytes=10 * 2**20),
        cost_estimate=pl.CostEstimate(flops=10**8, bytes_accessed=5 * 10**6, transcendentals=0),
        name="pick",
    )(turn, movers_row, key, inverse)


def simple(kernel, shapes, *args, specs=None, outs=None, limit=16 * 2**20, name=None):
    many = isinstance(shapes, (list, tuple))
    return pl.pallas_call(
        kernel,
        in_specs=specs or [VMEM] * len(args),
        out_specs=outs or ([VMEM] * len(shapes) if many else VMEM),
        out_shape=shapes,
        compiler_params=pltpu.CompilerParams(vmem_limit_bytes=limit),
        name=name,
    )(*args)


def shift(rows, columns):
    return [
        (y * SIDE + x, ((y + rows) % SIDE) * SIDE + (x + columns) % SIDE)
        for y in range(SIDE)
        for x in range(SIDE)
    ]


X_UP, X_DOWN, Y_UP, Y_DOWN = shift(0, 1), shift(0, -1), shift(1, 0), shift(-1, 0)


def send(x, pairs):
    return lax.ppermute(x, "col", pairs)


def ring_small(own, up, down):
    half = own.shape[0] // 2
    before = send(own, up)
    after = send(own, down)
    far = [send(before[:half], up), send(after[half:], down)]
    return jnp.stack([own, before, after, jnp.concatenate(far, axis=0)])


def ring_large(own, up, down):
    before = send(own, up)
    after = send(own, down)
    return [own, before, after, send(before[:2], up), send(after[2:], down)]


STEPS = (0, -1, 1, 2)


def where_is(outer, inner):
    if outer < 3:
        return outer, inner
    return 3 + inner // 2, inner % 2


def update_kernel(*refs):
    change_pieces, base_pieces = refs[0:5], refs[5:10]
    inverse, out_ref = refs[10:12]
    result, work, factors, combined, out_sems = refs[12:]
    own = lax.axis_index("col")
    own_y, own_x = own // SIDE, own % SIDE
    half = ALL // 2

    def blocks():
        for y in range(SIDE):
            for x in range(SIDE):
                block = ((own_y + STEPS[y] + SIDE) % SIDE) * SIDE + (
                    own_x + STEPS[x] + SIDE
                ) % SIDE
                rows = pl.ds(pl.multiple_of(block * BLOCK, BLOCK), BLOCK)
                by_row, by_column = where_is(y, x), where_is(x, y)
                yield block, rows, by_row, by_column

    def add(at, product, first):
        if first:
            work[at] = product
        else:
            work[at] = work[at] + product

    lower, upper = slice(0, half), slice(half, ALL)
    left, right = slice(0, ALL), slice(ALL, ALL + BLOCK)
    for number, (block, rows, by_row, by_column) in enumerate(blocks()):
        known = base_pieces[by_column[0]][by_column[1]]
        for part in (lower, upper):
            change = change_pieces[by_row[0]][by_row[1], part, :]
            add((part, left), jnp.dot(change, known, preferred_element_type=f32), number == 0)
    for number, (block, rows, by_row, by_column) in enumerate(blocks()):
        known = inverse[rows, :].astype(bf16)
        for part in (lower, upper):
            change = change_pieces[by_row[0]][by_row[1], part, :]
            add((part, right), jnp.dot(change, known, preferred_element_type=f32), number == 0)
    same = iota((K, K), 0) == iota((K, K), 1)
    identity = jnp.where(same, 1.0, 0.0).astype(f32)

    def split(value):
        high = value.astype(bf16)
        return high, (value - high.astype(f32)).astype(bf16)

    def multiply(one, other):
        def dot(left, right):
            return jnp.dot(left, right, preferred_element_type=f32)

        return dot(one[0], other[0]) + (dot(one[0], other[1]) + dot(one[1], other[0]))

    for window in range(ROUNDS):
        low, high = window * K, (window + 1) * K
        matrix = identity + work[low:high, low:high]
        matrix_parts = split(matrix)
        approx = 2.0 * identity - matrix
        for repeat in range(2):
            parts = split(approx)
            rest = 2.0 * identity - multiply(matrix_parts, parts)
            approx = multiply(parts, split(rest))
        factor = multiply(split(approx), split(work[low:high, :]))
        factors[low:high, :] = factor
        if window < ROUNDS - 1:
            work[high:, :] = work[high:, :] - multiply(
                split(work[high:, low:high]), split(factor)
            )
    for window in reversed(range(ROUNDS)):
        low, high = window * K, (window + 1) * K
        final = factors[low:high, ALL:]
        combined[low:high, :] = final.astype(bf16)
        if window:
            factors[:low, ALL:] = factors[:low, ALL:] - multiply(
                split(factors[:low, low:high]), split(final)
            )
    copies = []
    for number, (block, rows, by_row, by_column) in enumerate(blocks()):
        result[rows, :] = inverse[rows, :] - jnp.dot(
            base_pieces[by_column[0]][by_column[1]], combined[...], preferred_element_type=f32
        )
        copy = pltpu.make_async_copy(result.at[rows], out_ref.at[rows], out_sems.at[number])
        copy.start()
        copies.append(copy)
    for copy in copies:
        copy.wait()


def local(inverses, table, spots, groups, bricks, accept, movers, old_rows):
    inverse = inverses[0]
    sent, target, movers_row, key = simple(
        plan_kernel,
        [
            jax.ShapeDtypeStruct((SERVERS * CAP, 128), f32),
            jax.ShapeDtypeStruct((ALL, 128), jnp.int32),
            jax.ShapeDtypeStruct((1, ALL), jnp.int32),
            jax.ShapeDtypeStruct((ALL, 128), jnp.int32),
        ],
        groups.reshape(ROUNDS, 1, K),
        bricks,
        accept,
        movers,
        spots,
        limit=None,
        name="plan",
    )
    got = lax.all_to_all(
        sent.reshape(SERVERS, CAP, 128), "walker", split_axis=0, concat_axis=0, tiled=True
    ).reshape(SERVERS * CAP, 128)

    def share(turn):
        turn = turn.reshape(1)
        picked = pick(turn, movers_row, key, inverse)
        arrived = lax.all_to_all(picked, "col", split_axis=0, concat_axis=0, tiled=True)
        return simple(
            place_kernel,
            jax.ShapeDtypeStruct((BLOCK, ALL), bf16),
            turn,
            key,
            arrived.reshape(COLS * SHARE, BLOCK),
            specs=[SMEM, VMEM, VMEM],
            name="place",
        )

    answers, turns = simple(
        serve_kernel,
        [
            jax.ShapeDtypeStruct((SERVERS, SLOTS, BLOCK), bf16),
            jax.ShapeDtypeStruct((1,), jnp.int32),
        ],
        got,
        table.reshape(-1, BLOCK),
        outs=[VMEM, SMEM],
        name="serve",
    )
    base = share(jnp.int32(0))
    _, base = lax.while_loop(
        lambda state: state[0] < turns[0],
        lambda state: (state[0] + 1, state[1] + share(state[0])),
        (jnp.int32(1), base),
    )
    near_base = ring_small(base, Y_UP, Y_DOWN)
    answers = lax.all_to_all(answers, "walker", split_axis=0, concat_axis=0, tiled=True)
    change = simple(
        collect_kernel,
        jax.ShapeDtypeStruct((ALL, BLOCK), bf16),
        target,
        answers.reshape(SERVERS * SLOTS, BLOCK),
        old_rows.reshape(ALL, BLOCK),
        name="collect",
    )
    near_change = ring_small(change, X_UP, X_DOWN)
    near_base, near_change = lax.optimization_barrier((near_base, near_change))
    change_pieces = ring_large(near_change, Y_UP, Y_DOWN)
    base_pieces = ring_large(near_base, X_UP, X_DOWN)
    updated = pl.pallas_call(
        update_kernel,
        in_specs=[VMEM] * 11,
        out_specs=ANY,
        out_shape=jax.ShapeDtypeStruct((N, BLOCK), f32),
        scratch_shapes=[
            pltpu.VMEM((N, BLOCK), f32),
            pltpu.VMEM((ALL, ALL + BLOCK), f32),
            pltpu.VMEM((ALL, ALL + BLOCK), f32),
            pltpu.VMEM((ALL, BLOCK), bf16),
            pltpu.SemaphoreType.DMA((COLS,)),
        ],
        compiler_params=pltpu.CompilerParams(vmem_limit_bytes=26 * 2**20),
        name="update",
    )(*change_pieces, *base_pieces, inverse)
    return updated[None]


def solution(mesh):
    return jax.shard_map(
        local,
        mesh=mesh,
        in_specs=(
            P("walker", None, "col"),
            P("walker", None, "col"),
            P(None, None, "walker", None),
            P(None, "walker", None, None),
            P(None, "walker", None),
            P(None, "walker", None),
            P(None, "walker", None),
            P(None, "walker", None, "col"),
        ),
        out_specs=P("walker", None, "col"),
        check_vma=False,
    )
```

profile of v0, /device:TPU:24, one launch (start us, length us, event | category | flops | bytes accessed | tf_op | source)
XLA Modules:
  0.0 116.7 jit_solution(9829346551600052793)
XLA Ops:
  0.0 2.6 %plan.1 = (f32[128,128]{1,0:T(8,128)}, s32[384,128]{1,0:T(8,128)}, s32[1,384]{1,0:T(1,128)S(1)}, s32[384,128]{1,0:T(8,128)S(1)}) custom-call(s32[6,1,64]{2,1,0:T(1,128)} %bitcast.42, s32[6,1,64]{2,1,0:T(1,128)} %bricks_ref.1, s32[6,1,64]{2,1,0:T(1,128)} %accept_ref.1, s32[6,1,64]{2,1,0:T(1,128)} %movers_ref.1, f32[3,6,1,64]{3,2,1,0:T(1,128)} %spots_ref.1), custom_call_target="tpu_custom_call" | custom-call | tf_op jit(solution)/shard_map/plan/pallas_call | solution.py:198
  2.6 8.6 %all-to-all-start.2 = ((f32[16,8,128]{2,1,0:T(8,128)}), f32[16,8,128]{2,1,0:T(8,128)S(1)}, u32[]{:S(2)}, u32[]{:S(2)}) async-start(f32[16,8,128]{2,1,0:T(8,128)} %bitcast.41), calls=%async_computation.2 | async-start | bytes 131072 | tf_op jit(solution)/shard_map/all_to_all | solution.py:348
  11.2 4.7 %pick.2 = bf16[16,48,256]{2,1,0:T(8,128)(2,1)} custom-call(s32[1]{0:T(128)} %constant.2.clone.1.turn_ref, s32[1,384]{1,0:T(1,128)S(1)} %get-tuple-element.108.movers_ref, s32[384,128]{1,0:T(8,128)S(1)} %get-tuple-element.109.key_ref, f32[4096,256]{1,0:T(8,128)} %bitcast.34), custom_call_target="tpu_custom_call" | custom-call | flops 100000000 | bytes 5000000 | tf_op jit(solution)/shard_map/pick/pallas_call | solution.py:178
  16.0 3.1 %all-to-all-done.2 = f32[16,8,128]{2,1,0:T(8,128)S(1)} async-done(((f32[16,8,128]{2,1,0:T(8,128)}), f32[16,8,128]{2,1,0:T(8,128)S(1)}, u32[]{:S(2)}, u32[]{:S(2)}) %all-to-all-start.2) | async-done | bytes 65568 | tf_op jit(solution)/shard_map/all_to_all | solution.py:348
  19.0 7.2 %all-to-all-start.1 = ((bf16[16,48,256]{2,1,0:T(8,128)(2,1)}), bf16[16,48,256]{2,1,0:T(8,128)(2,1)S(1)}, u32[]{:S(2)}, u32[]{:S(2)}) async-start(bf16[16,48,256]{2,1,0:T(8,128)(2,1)} %pick.2), calls=%async_computation.1 | async-start | bytes 786432 | tf_op jit(solution)/shard_map/all_to_all | solution.py:355
  26.2 2.6 %serve.1 = (bf16[16,48,256]{2,1,0:T(8,128)(2,1)}, s32[1]{0:T(128)}) custom-call(f32[128,128]{1,0:T(8,128)S(1)} %bitcast.32, bf16[2048,256]{1,0:T(8,128)(2,1)S(1)} %bitcast.30), custom_call_target="tpu_custom_call" | custom-call | tf_op jit(solution)/shard_map/serve/pallas_call | solution.py:198
  28.8 5.8 %all-to-all-done.1 = bf16[16,48,256]{2,1,0:T(8,128)(2,1)S(1)} async-done(((bf16[16,48,256]{2,1,0:T(8,128)(2,1)}), bf16[16,48,256]{2,1,0:T(8,128)(2,1)S(1)}, u32[]{:S(2)}, u32[]{:S(2)}) %all-to-all-start.1) | async-done | bytes 393248 | tf_op jit(solution)/shard_map/all_to_all | solution.py:355
  34.5 0.5 place.2
  35.1 0.7 while.10
  35.8 3.9 %all-to-all-start.3 = ((bf16[16,48,256]{2,1,0:T(8,128)(2,1)}), bf16[16,48,256]{2,1,0:T(8,128)(2,1)S(1)}, u32[]{:S(2)}, u32[]{:S(2)}) async-start(bf16[16,48,256]{2,1,0:T(8,128)(2,1)} %get-tuple-element.52), calls=%async_computation.3 | async-start | bytes 786432 | tf_op jit(solution)/shard_map/all_to_all | solution.py:384
  39.7 2.5 %collective-permute-start = (bf16[256,384]{1,0:T(8,128)(2,1)S(1)}, bf16[256,384]{1,0:T(8,128)(2,1)S(1)}, u32[]{:S(2)}, u32[]{:S(2)}) collective-permute-start(bf16[256,384]{1,0:T(8,128)(2,1)S(1)} %get-tuple-element.50), channel_id=1, source_target_pairs={{0,4},{1,5},{2,6},{3,7},{4,8},{5,9},{6,10},{7,11},{8,12},{9,13},{1... | collective-permute-start | bytes 589832 | tf_op jit(solution)/shard_map/ppermute | solution.py:220
  42.1 4.8 %collective-permute-done = bf16[256,384]{1,0:T(8,128)(2,1)S(1)} collective-permute-done((bf16[256,384]{1,0:T(8,128)(2,1)S(1)}, bf16[256,384]{1,0:T(8,128)(2,1)S(1)}, u32[]{:S(2)}, u32[]{:S(2)}) %collective-permute-start) | collective-permute-done | bytes 196640 | tf_op jit(solution)/shard_map/ppermute | solution.py:220
  46.9 3.7 %collective-permute-start.2 = (bf16[128,384]{1,0:T(8,128)(2,1)S(1)}, bf16[128,384]{1,0:T(8,128)(2,1)S(1)}, u32[]{:S(2)}, u32[]{:S(2)}) collective-permute-start(bf16[128,384]{1,0:T(8,128)(2,1)S(1)} %slice.32), channel_id=1, source_target_pairs={{0,4},{1,5},{2,6},{3,7},{4,8},{5,9},{6,10},{7,11},{8,12},{9,13},{1... | collective-permute-start | bytes 294920 | tf_op jit(solution)/shard_map/ppermute | solution.py:220
  50.7 2.6 %all-to-all-done.3 = bf16[16,48,256]{2,1,0:T(8,128)(2,1)S(1)} async-done(((bf16[16,48,256]{2,1,0:T(8,128)(2,1)}), bf16[16,48,256]{2,1,0:T(8,128)(2,1)S(1)}, u32[]{:S(2)}, u32[]{:S(2)}) %all-to-all-start.3) | async-done | bytes 393248 | tf_op jit(solution)/shard_map/all_to_all | solution.py:384
  53.3 0.4 collect.1
  53.7 1.0 collective-permute-start.5
  54.7 1.1 collective-permute-start.4
  55.8 0.7 collective-permute-done.3
  56.5 4.7 %collective-permute-done.5 = bf16[384,256]{1,0:T(8,128)(2,1)S(1)} collective-permute-done((bf16[384,256]{1,0:T(8,128)(2,1)S(1)}, bf16[384,256]{1,0:T(8,128)(2,1)S(1)}, u32[]{:S(2)}, u32[]{:S(2)}) %collective-permute-start.5) | collective-permute-done | bytes 196640 | tf_op jit(solution)/shard_map/ppermute | solution.py:220
  61.3 2.2 %collective-permute-start.7 = (bf16[192,256]{1,0:T(8,128)(2,1)S(1)}, bf16[192,256]{1,0:T(8,128)(2,1)S(1)}, u32[]{:S(2)}, u32[]{:S(2)}) collective-permute-start(bf16[192,256]{1,0:T(8,128)(2,1)S(1)} %slice.35), channel_id=1, source_target_pairs={{0,3},{1,0},{2,1},{3,2},{4,7},{5,4},{6,5},{7,6},{8,11},{9,8},{10,9... | collective-permute-start | bytes 294920 | tf_op jit(solution)/shard_map/ppermute | solution.py:220
  64.1 2.4 %collective-permute-done.7 = bf16[192,256]{1,0:T(8,128)(2,1)S(1)} collective-permute-done((bf16[192,256]{1,0:T(8,128)(2,1)S(1)}, bf16[192,256]{1,0:T(8,128)(2,1)S(1)}, u32[]{:S(2)}, u32[]{:S(2)}) %collective-permute-start.7) | collective-permute-done | bytes 98336 | tf_op jit(solution)/shard_map/ppermute | solution.py:220
  66.5 3.5 %collective-permute-done.6 = bf16[192,256]{1,0:T(8,128)(2,1)S(1)} collective-permute-done((bf16[192,256]{1,0:T(8,128)(2,1)S(1)}, bf16[192,256]{1,0:T(8,128)(2,1)S(1)}, u32[]{:S(2)}, u32[]{:S(2)}) %collective-permute-start.6) | collective-permute-done | bytes 98336 | tf_op jit(solution)/shard_map/ppermute | solution.py:220
  70.1 0.9 collective-permute-start.9
  71.0 2.4 %collective-permute-start.8 = (bf16[4,384,256]{2,1,0:T(8,128)(2,1)S(1)}, bf16[4,384,256]{2,1,0:T(8,128)(2,1)S(1)}, u32[]{:S(2)}, u32[]{:S(2)}) collective-permute-start(bf16[4,384,256]{2,1,0:T(8,128)(2,1)S(1)} %pad_maximum_fusion.1.refs_0_), channel_id=1, source_target_pairs={{0,4},{1,5},{2,6},{3,7},{4,8},{5,9},{6,10},{7,11},{8,12},{9,13},{1... | collective-permute-start | bytes 2359304 | tf_op jit(solution)/shard_map/ppermute | solution.py:220
  73.4 2.0 %collective-permute-start.12 = (bf16[4,256,384]{2,1,0:T(8,128)(2,1)S(1)}, bf16[4,256,384]{2,1,0:T(8,128)(2,1)S(1)}, u32[]{:S(2)}, u32[]{:S(2)}) collective-permute-start(bf16[4,256,384]{2,1,0:T(8,128)(2,1)S(1)} %pad_maximum_fusion.refs_5_), channel_id=1, source_target_pairs={{0,1},{1,2},{2,3},{3,0},{4,5},{5,6},{6,7},{7,4},{8,9},{9,10},{10,1... | collective-permute-start | bytes 2359304 | tf_op jit(solution)/shard_map/ppermute | solution.py:220
  75.4 14.7 %collective-permute-done.9.refs_2_ = bf16[4,384,256]{2,1,0:T(8,128)(2,1)S(1)} collective-permute-done((bf16[4,384,256]{2,1,0:T(8,128)(2,1)S(1)}, bf16[4,384,256]{2,1,0:T(8,128)(2,1)S(1)}, u32[]{:S(2)}, u32[]{:S(2)}) %collective-permute-start.9) | collective-permute-done | bytes 786464 | tf_op jit(solution)/shard_map/ppermute | solution.py:220
  90.2 3.3 %collective-permute-start.10 = (bf16[2,384,256]{2,1,0:T(8,128)(2,1)S(1)}, bf16[2,384,256]{2,1,0:T(8,128)(2,1)S(1)}, u32[]{:S(2)}, u32[]{:S(2)}) collective-permute-start(bf16[2,384,256]{2,1,0:T(8,128)(2,1)S(1)} %slice.36), channel_id=1, source_target_pairs={{0,4},{1,5},{2,6},{3,7},{4,8},{5,9},{6,10},{7,11},{8,12},{9,13},{1... | collective-permute-start | bytes 1179656 | tf_op jit(solution)/shard_map/ppermute | solution.py:220
  93.7 2.3 %collective-permute-start.14 = (bf16[2,256,384]{2,1,0:T(8,128)(2,1)S(1)}, bf16[2,256,384]{2,1,0:T(8,128)(2,1)S(1)}, u32[]{:S(2)}, u32[]{:S(2)}) collective-permute-start(bf16[2,256,384]{2,1,0:T(8,128)(2,1)S(1)} %slice.38), channel_id=1, source_target_pairs={{0,1},{1,2},{2,3},{3,0},{4,5},{5,6},{6,7},{7,4},{8,9},{9,10},{10,1... | collective-permute-start | bytes 1179656 | tf_op jit(solution)/shard_map/ppermute | solution.py:220
  96.0 4.8 %collective-permute-done.11.refs_4_ = bf16[2,384,256]{2,1,0:T(8,128)(2,1)S(1)} collective-permute-done((bf16[2,384,256]{2,1,0:T(8,128)(2,1)S(1)}, bf16[2,384,256]{2,1,0:T(8,128)(2,1)S(1)}, u32[]{:S(2)}, u32[]{:S(2)}) %collective-permute-start.11) | collective-permute-done | bytes 393248 | tf_op jit(solution)/shard_map/ppermute | solution.py:220
  100.8 1.7 %collective-permute-done.15.refs_9_ = bf16[2,256,384]{2,1,0:T(8,128)(2,1)S(1)} collective-permute-done((bf16[2,256,384]{2,1,0:T(8,128)(2,1)S(1)}, bf16[2,256,384]{2,1,0:T(8,128)(2,1)S(1)}, u32[]{:S(2)}, u32[]{:S(2)}) %collective-permute-start.15) | collective-permute-done | bytes 393248 | tf_op jit(solution)/shard_map/ppermute | solution.py:220
  102.5 1.6 %collective-permute-done.14.refs_8_ = bf16[2,256,384]{2,1,0:T(8,128)(2,1)S(1)} collective-permute-done((bf16[2,256,384]{2,1,0:T(8,128)(2,1)S(1)}, bf16[2,256,384]{2,1,0:T(8,128)(2,1)S(1)}, u32[]{:S(2)}, u32[]{:S(2)}) %collective-permute-start.14) | collective-permute-done | bytes 393248 | tf_op jit(solution)/shard_map/ppermute | solution.py:220
  104.1 12.5 %update.1 = f32[4096,256]{1,0:T(8,128)} custom-call(bf16[4,384,256]{2,1,0:T(8,128)(2,1)S(1)} %pad_maximum_fusion.1.refs_0_, bf16[4,384,256]{2,1,0:T(8,128)(2,1)S(1)} %collective-permute-done.8.refs_1_, bf16[4,384,256]{2,1,0:T(8,128)(2,1)S(1)} %collective-permute-done.9.refs_2_, bf16[2,384,256]{2,1,0:T(8,128)(2,1)S(1)} %collective-permute-done.10.refs_3_, ...), custom_call_target="tpu_custom_call" | custom-call | tf_op jit(solution)/shard_map/update/pallas_call | solution.py:397
  (33 shorter events, 1.2 us)
Async XLA Ops:
  0.0 26.2 %copy-start = (bf16[32,64,256]{2,1,0:T(8,128)(2,1)S(1)}, bf16[32,64,256]{2,1,0:T(8,128)(2,1)}, u32[]{:S(2)}) copy-start(bf16[32,64,256]{2,1,0:T(8,128)(2,1)} %param.11) | copy-start | bytes 3145732
  2.6 16.4 %all-to-all-start.2 = ((f32[16,8,128]{2,1,0:T(8,128)}), f32[16,8,128]{2,1,0:T(8,128)S(1)}, u32[]{:S(2)}, u32[]{:S(2)}) async-start(f32[16,8,128]{2,1,0:T(8,128)} %bitcast.41), calls=%async_computation.2 | async-start | bytes 131072 | tf_op jit(solution)/shard_map/all_to_all | solution.py:348
  19.0 15.5 %all-to-all-start.1 = ((bf16[16,48,256]{2,1,0:T(8,128)(2,1)}), bf16[16,48,256]{2,1,0:T(8,128)(2,1)S(1)}, u32[]{:S(2)}, u32[]{:S(2)}) async-start(bf16[16,48,256]{2,1,0:T(8,128)(2,1)} %pick.2), calls=%async_computation.1 | async-start | bytes 786432 | tf_op jit(solution)/shard_map/all_to_all | solution.py:355
  35.1 18.2 %copy-start.1 = (bf16[6,1,64,256]{3,2,1,0:T(8,128)(2,1)S(1)}, bf16[6,1,64,256]{3,2,1,0:T(8,128)(2,1)}, u32[]{:S(2)}) copy-start(bf16[6,1,64,256]{3,2,1,0:T(8,128)(2,1)} %param.17) | copy-start | bytes 589828
  35.1 18.2 %copy-start.2 = (s32[384,128]{1,0:T(8,128)S(1)}, s32[384,128]{1,0:T(8,128)}, u32[]{:S(2)}) copy-start(s32[384,128]{1,0:T(8,128)} %get-tuple-element.51.target_ref) | copy-start | bytes 589828
  35.8 17.5 %all-to-all-start.3 = ((bf16[16,48,256]{2,1,0:T(8,128)(2,1)}), bf16[16,48,256]{2,1,0:T(8,128)(2,1)S(1)}, u32[]{:S(2)}, u32[]{:S(2)}) async-start(bf16[16,48,256]{2,1,0:T(8,128)(2,1)} %get-tuple-element.52), calls=%async_computation.3 | async-start | bytes 786432 | tf_op jit(solution)/shard_map/all_to_all | solution.py:384
  39.7 7.2 %collective-permute-start = (bf16[256,384]{1,0:T(8,128)(2,1)S(1)}, bf16[256,384]{1,0:T(8,128)(2,1)S(1)}, u32[]{:S(2)}, u32[]{:S(2)}) collective-permute-start(bf16[256,384]{1,0:T(8,128)(2,1)S(1)} %get-tuple-element.50), channel_id=1, source_target_pairs={{0,4},{1,5},{2,6},{3,7},{4,8},{5,9},{6,10},{7,11},{8,12},{9,13},{1... | collective-permute-start | bytes 589832 | tf_op jit(solution)/shard_map/ppermute | solution.py:220
  42.1 8.4 %collective-permute-start.1 = (bf16[256,384]{1,0:T(8,128)(2,1)S(1)}, bf16[256,384]{1,0:T(8,128)(2,1)S(1)}, u32[]{:S(2)}, u32[]{:S(2)}) collective-permute-start(bf16[256,384]{1,0:T(8,128)(2,1)S(1)} %get-tuple-element.50), channel_id=1, source_target_pairs={{0,12},{1,13},{2,14},{3,15},{4,0},{5,1},{6,2},{7,3},{8,4},{9,5},{1... | collective-permute-start | bytes 589832 | tf_op jit(solution)/shard_map/ppermute | solution.py:220
  46.9 8.9 %collective-permute-start.2 = (bf16[128,384]{1,0:T(8,128)(2,1)S(1)}, bf16[128,384]{1,0:T(8,128)(2,1)S(1)}, u32[]{:S(2)}, u32[]{:S(2)}) collective-permute-start(bf16[128,384]{1,0:T(8,128)(2,1)S(1)} %slice.32), channel_id=1, source_target_pairs={{0,4},{1,5},{2,6},{3,7},{4,8},{5,9},{6,10},{7,11},{8,12},{9,13},{1... | collective-permute-start | bytes 294920 | tf_op jit(solution)/shard_map/ppermute | solution.py:220
  50.6 5.9 %collective-permute-start.3 = (bf16[128,384]{1,0:T(8,128)(2,1)S(1)}, bf16[128,384]{1,0:T(8,128)(2,1)S(1)}, u32[]{:S(2)}, u32[]{:S(2)}) collective-permute-start(bf16[128,384]{1,0:T(8,128)(2,1)S(1)} %slice.33), channel_id=1, source_target_pairs={{0,12},{1,13},{2,14},{3,15},{4,0},{5,1},{6,2},{7,3},{8,4},{9,5},{1... | collective-permute-start | bytes 294920 | tf_op jit(solution)/shard_map/ppermute | solution.py:220
  53.3 50.8 %copy-start.3 = (f32[4096,256]{1,0:T(8,128)S(1)}, f32[4096,256]{1,0:T(8,128)}, u32[]{:S(2)}) copy-start(f32[4096,256]{1,0:T(8,128)} %get-tuple-element.144) | copy-start | bytes 12582916
  53.7 7.6 %collective-permute-start.5 = (bf16[384,256]{1,0:T(8,128)(2,1)S(1)}, bf16[384,256]{1,0:T(8,128)(2,1)S(1)}, u32[]{:S(2)}, u32[]{:S(2)}) collective-permute-start(bf16[384,256]{1,0:T(8,128)(2,1)S(1)} %collect.1), channel_id=1, source_target_pairs={{0,3},{1,0},{2,1},{3,2},{4,7},{5,4},{6,5},{7,6},{8,11},{9,8},{10,9... | collective-permute-start | bytes 589832 | tf_op jit(solution)/shard_map/ppermute | solution.py:220
  54.7 9.0 %collective-permute-start.4 = (bf16[384,256]{1,0:T(8,128)(2,1)S(1)}, bf16[384,256]{1,0:T(8,128)(2,1)S(1)}, u32[]{:S(2)}, u32[]{:S(2)}) collective-permute-start(bf16[384,256]{1,0:T(8,128)(2,1)S(1)} %collect.1), channel_id=1, source_target_pairs={{0,1},{1,2},{2,3},{3,0},{4,5},{5,6},{6,7},{7,4},{8,9},{9,10},{10,1... | collective-permute-start | bytes 589832 | tf_op jit(solution)/shard_map/ppermute | solution.py:220
  61.3 5.2 %collective-permute-start.7 = (bf16[192,256]{1,0:T(8,128)(2,1)S(1)}, bf16[192,256]{1,0:T(8,128)(2,1)S(1)}, u32[]{:S(2)}, u32[]{:S(2)}) collective-permute-start(bf16[192,256]{1,0:T(8,128)(2,1)S(1)} %slice.35), channel_id=1, source_target_pairs={{0,3},{1,0},{2,1},{3,2},{4,7},{5,4},{6,5},{7,6},{8,11},{9,8},{10,9... | collective-permute-start | bytes 294920 | tf_op jit(solution)/shard_map/ppermute | solution.py:220
  63.6 6.3 %collective-permute-start.6 = (bf16[192,256]{1,0:T(8,128)(2,1)S(1)}, bf16[192,256]{1,0:T(8,128)(2,1)S(1)}, u32[]{:S(2)}, u32[]{:S(2)}) collective-permute-start(bf16[192,256]{1,0:T(8,128)(2,1)S(1)} %slice.34), channel_id=1, source_target_pairs={{0,1},{1,2},{2,3},{3,0},{4,5},{5,6},{6,7},{7,4},{8,9},{9,10},{10,1... | collective-permute-start | bytes 294920 | tf_op jit(solution)/shard_map/ppermute | solution.py:220
  70.1 20.0 %collective-permute-start.9 = (bf16[4,384,256]{2,1,0:T(8,128)(2,1)S(1)}, bf16[4,384,256]{2,1,0:T(8,128)(2,1)S(1)}, u32[]{:S(2)}, u32[]{:S(2)}) collective-permute-start(bf16[4,384,256]{2,1,0:T(8,128)(2,1)S(1)} %pad_maximum_fusion.1.refs_0_), channel_id=1, source_target_pairs={{0,12},{1,13},{2,14},{3,15},{4,0},{5,1},{6,2},{7,3},{8,4},{9,5},{1... | collective-permute-start | bytes 2359304 | tf_op jit(solution)/shard_map/ppermute | solution.py:220
  71.0 19.2 %collective-permute-start.8 = (bf16[4,384,256]{2,1,0:T(8,128)(2,1)S(1)}, bf16[4,384,256]{2,1,0:T(8,128)(2,1)S(1)}, u32[]{:S(2)}, u32[]{:S(2)}) collective-permute-start(bf16[4,384,256]{2,1,0:T(8,128)(2,1)S(1)} %pad_maximum_fusion.1.refs_0_), channel_id=1, source_target_pairs={{0,4},{1,5},{2,6},{3,7},{4,8},{5,9},{6,10},{7,11},{8,12},{9,13},{1... | collective-permute-start | bytes 2359304 | tf_op jit(solution)/shard_map/ppermute | solution.py:220
  73.4 20.1 %collective-permute-start.13 = (bf16[4,256,384]{2,1,0:T(8,128)(2,1)S(1)}, bf16[4,256,384]{2,1,0:T(8,128)(2,1)S(1)}, u32[]{:S(2)}, u32[]{:S(2)}) collective-permute-start(bf16[4,256,384]{2,1,0:T(8,128)(2,1)S(1)} %pad_maximum_fusion.refs_5_), channel_id=1, source_target_pairs={{0,3},{1,0},{2,1},{3,2},{4,7},{5,4},{6,5},{7,6},{8,11},{9,8},{10,9... | collective-permute-start | bytes 2359304 | tf_op jit(solution)/shard_map/ppermute | solution.py:220
  73.4 20.3 %collective-permute-start.12 = (bf16[4,256,384]{2,1,0:T(8,128)(2,1)S(1)}, bf16[4,256,384]{2,1,0:T(8,128)(2,1)S(1)}, u32[]{:S(2)}, u32[]{:S(2)}) collective-permute-start(bf16[4,256,384]{2,1,0:T(8,128)(2,1)S(1)} %pad_maximum_fusion.refs_5_), channel_id=1, source_target_pairs={{0,1},{1,2},{2,3},{3,0},{4,5},{5,6},{6,7},{7,4},{8,9},{9,10},{10,1... | collective-permute-start | bytes 2359304 | tf_op jit(solution)/shard_map/ppermute | solution.py:220
  90.1 10.7 %collective-permute-start.11 = (bf16[2,384,256]{2,1,0:T(8,128)(2,1)S(1)}, bf16[2,384,256]{2,1,0:T(8,128)(2,1)S(1)}, u32[]{:S(2)}, u32[]{:S(2)}) collective-permute-start(bf16[2,384,256]{2,1,0:T(8,128)(2,1)S(1)} %slice.37), channel_id=1, source_target_pairs={{0,12},{1,13},{2,14},{3,15},{4,0},{5,1},{6,2},{7,3},{8,4},{9,5},{1... | collective-permute-start | bytes 1179656 | tf_op jit(solution)/shard_map/ppermute | solution.py:220
  90.2 10.6 %collective-permute-start.10 = (bf16[2,384,256]{2,1,0:T(8,128)(2,1)S(1)}, bf16[2,384,256]{2,1,0:T(8,128)(2,1)S(1)}, u32[]{:S(2)}, u32[]{:S(2)}) collective-permute-start(bf16[2,384,256]{2,1,0:T(8,128)(2,1)S(1)} %slice.36), channel_id=1, source_target_pairs={{0,4},{1,5},{2,6},{3,7},{4,8},{5,9},{6,10},{7,11},{8,12},{9,13},{1... | collective-permute-start | bytes 1179656 | tf_op jit(solution)/shard_map/ppermute | solution.py:220
  93.6 8.9 %collective-permute-start.15 = (bf16[2,256,384]{2,1,0:T(8,128)(2,1)S(1)}, bf16[2,256,384]{2,1,0:T(8,128)(2,1)S(1)}, u32[]{:S(2)}, u32[]{:S(2)}) collective-permute-start(bf16[2,256,384]{2,1,0:T(8,128)(2,1)S(1)} %slice.39), channel_id=1, source_target_pairs={{0,3},{1,0},{2,1},{3,2},{4,7},{5,4},{6,5},{7,6},{8,11},{9,8},{10,9... | collective-permute-start | bytes 1179656 | tf_op jit(solution)/shard_map/ppermute | solution.py:220
  93.7 10.4 %collective-permute-start.14 = (bf16[2,256,384]{2,1,0:T(8,128)(2,1)S(1)}, bf16[2,256,384]{2,1,0:T(8,128)(2,1)S(1)}, u32[]{:S(2)}, u32[]{:S(2)}) collective-permute-start(bf16[2,256,384]{2,1,0:T(8,128)(2,1)S(1)} %slice.38), channel_id=1, source_target_pairs={{0,1},{1,2},{2,3},{3,0},{4,5},{5,6},{6,7},{7,4},{8,9},{9,10},{10,1... | collective-permute-start | bytes 1179656 | tf_op jit(solution)/shard_map/ppermute | solution.py:220
where the time goes:
time: 117 us
  waiting for transfers between devices  50.4 us (43%)
  starting transfers between devices  41.5 us (35%)
  Pallas kernels  23.3 us (20%)
    ppermute x16, waiting for transfers between devices, send(): return lax.ppermute(x, 'col', pairs)  39 us
    ppermute x16, starting transfers between devices, send(): return lax.ppermute(x, 'col', pairs)  21.8 us
    pallas_call x1, Pallas kernels, local(): pl.pallas_call(update_kernel, in_specs=[VMEM] * 11, out_specs=ANY, out_sh...  12.5 us
    all_to_all x1, starting transfers between devices, local(): lax.all_to_all(sent.reshape(SERVERS, CAP, 128), 'walker', split_axis=0, c...  8.57 us
    all_to_all x1, starting transfers between devices, share(): lax.all_to_all(picked, 'col', split_axis=0, concat_axis=0, tiled=True)  7.17 us
    pallas_call x4, Pallas kernels, simple(): pl.pallas_call(kernel, in_specs=specs or [VMEM] * len(args), out_specs=ou...  6.12 us
    all_to_all x1, waiting for transfers between devices, share(): lax.all_to_all(picked, 'col', split_axis=0, concat_axis=0, tiled=True)  5.78 us
    pallas_call x1, Pallas kernels, pick(): pl.pallas_call(pick_kernel, grid=(COLS // step,), in_specs=[SMEM, pl.Bloc...  4.73 us
  transfers between devices with their start and end apart: 19, of which 13 were waited for; matrix products, arithmetic and copies ran while one was open for 0% of the time, Pallas kernels for 7%

commit v1 on v0

--- a/solution.py
+++ b/solution.py
@@ -4,6 +4,7 @@
 from jax.experimental import pallas as pl
 from jax.experimental.pallas import tpu as pltpu
 from jax.sharding import PartitionSpec as P
+
 
 N = 4096
 K = 64
@@ -105,6 +106,7 @@
         def column(field):
             at = 8 * window + field
             return jnp.broadcast_to(got_ref[:, at : at + 1], (rows, 128))
+
         weight = (
             basis_at(column(0), point // 16)
             * basis_at(column(1), (point // 4) % 4)
@@ -155,14 +157,24 @@
     picked = lax.dot_general(
         chosen[...], inverse_ref[...].astype(bf16), NT, preferred_element_type=f32
     ).astype(bf16)
-    for piece in range(out_ref.shape[0]):
-        out_ref[piece] = picked[:, piece * BLOCK : (piece + 1) * BLOCK]
-
-
-def place_kernel(turn_ref, key_ref, got_ref, out_ref):
+    own = lax.axis_index("col")
+    for piece in range(SIDE):
+        columns = (piece - own % SIDE + SIDE) % SIDE
+        rows = (pl.program_id(0) - own // SIDE + SIDE) % SIDE
+        out_ref[columns, rows] = picked[:, piece * BLOCK : (piece + 1) * BLOCK]
+
+
+def place_kernel(turn_ref, key_ref, *refs):
+    got_refs, out_ref = refs[:SIDE], refs[SIDE]
+    own = lax.axis_index("col")
     key = key_ref[...]
     rank = key % ALL - turn_ref[0] * SHARE
-    spot = jnp.where((rank >= 0) & (rank < SHARE), (key // ALL) * SHARE + rank, -1)
+    owner = key // ALL
+    rows = (own // SIDE - owner // SIDE + SIDE) % SIDE
+    columns = (own % SIDE - owner % SIDE + SIDE) % SIDE
+    spot = jnp.where(
+        (rank >= 0) & (rank < SHARE), (rows * SIDE + columns) * SHARE + rank, -1
+    )
     onehot = jnp.concatenate(
         [
             jnp.where(spot == piece * 128 + iota((ALL, 128), 1), 1.0, 0.0).astype(bf16)
@@ -170,22 +182,25 @@
         ],
         axis=1,
     )
-    out_ref[...] = jnp.dot(onehot, got_ref[...], preferred_element_type=f32).T.astype(bf16)
+    out_ref[...] = jnp.dot(
+        onehot,
+        jnp.concatenate([ref[...] for ref in got_refs], axis=0),
+        preferred_element_type=f32,
+    ).T.astype(bf16)
 
 
 def pick(turn, movers_row, key, inverse):
-    step = 4
     return pl.pallas_call(
         pick_kernel,
-        grid=(COLS // step,),
+        grid=(SIDE,),
         in_specs=[
             SMEM,
             pl.BlockSpec((1, ALL), lambda i: (0, 0)),
             pl.BlockSpec((ALL, 128), lambda i: (0, 0)),
-            pl.BlockSpec((step * BLOCK, BLOCK), lambda i: (i, 0)),
-        ],
-        out_specs=pl.BlockSpec((step, SHARE, BLOCK), lambda i: (i, 0, 0)),
-        out_shape=jax.ShapeDtypeStruct((COLS, SHARE, BLOCK), bf16),
+            pl.BlockSpec((SIDE * BLOCK, BLOCK), lambda i: (i, 0)),
+        ],
+        out_specs=pl.BlockSpec((SIDE, SIDE, SHARE, BLOCK), lambda i: (0, 0, 0, 0)),
+        out_shape=jax.ShapeDtypeStruct((SIDE, SIDE, SHARE, BLOCK), bf16),
         scratch_shapes=[pltpu.VMEM((SHARE, BLOCK), bf16)],
         compiler_params=pltpu.CompilerParams(vmem_limit_bytes=10 * 2**20),
         cost_estimate=pl.CostEstimate(flops=10**8, bytes_accessed=5 * 10**6, transcendentals=0),
@@ -193,7 +208,7 @@
     )(turn, movers_row, key, inverse)
 
 
-def simple(kernel, shapes, *args, specs=None, outs=None, limit=16 * 2**20, name=None):
+def simple(kernel, shapes, *args, specs=None, outs=None, limit=16 * 2**20):
     many = isinstance(shapes, (list, tuple))
     return pl.pallas_call(
         kernel,
@@ -201,7 +216,6 @@
         out_specs=outs or ([VMEM] * len(shapes) if many else VMEM),
         out_shape=shapes,
         compiler_params=pltpu.CompilerParams(vmem_limit_bytes=limit),
-        name=name,
     )(*args)
 
 
@@ -297,7 +311,7 @@
         matrix = identity + work[low:high, low:high]
         matrix_parts = split(matrix)
         approx = 2.0 * identity - matrix
-        for repeat in range(2):
+        for _ in range(2):
             parts = split(approx)
             rest = 2.0 * identity - multiply(matrix_parts, parts)
             approx = multiply(parts, split(rest))
@@ -343,24 +357,32 @@
         movers,
         spots,
         limit=None,
-        name="plan",
     )
     got = lax.all_to_all(
         sent.reshape(SERVERS, CAP, 128), "walker", split_axis=0, concat_axis=0, tiled=True
     ).reshape(SERVERS * CAP, 128)
 
-    def share(turn):
+    def share(turn, after=None):
         turn = turn.reshape(1)
         picked = pick(turn, movers_row, key, inverse)
-        arrived = lax.all_to_all(picked, "col", split_axis=0, concat_axis=0, tiled=True)
+        if after is not None:
+            picked, after = lax.optimization_barrier((picked, after))
+        across = [picked[0]]
+        for step in range(1, SIDE):
+            across.append(send(picked[step], shift(0, step)))
+        down = []
+        for step in range(SIDE):
+            block = jnp.stack([part[step] for part in across])
+            if step:
+                block = send(block, shift(step, 0))
+            down.append(block.reshape(SIDE * SHARE, BLOCK))
         return simple(
             place_kernel,
             jax.ShapeDtypeStruct((BLOCK, ALL), bf16),
             turn,
             key,
-            arrived.reshape(COLS * SHARE, BLOCK),
-            specs=[SMEM, VMEM, VMEM],
-            name="place",
+            *down,
+            specs=[SMEM] + [VMEM] * (1 + SIDE),
         )
 
     answers, turns = simple(
@@ -372,15 +394,13 @@
         got,
         table.reshape(-1, BLOCK),
         outs=[VMEM, SMEM],
-        name="serve",
-    )
-    base = share(jnp.int32(0))
+    )
+    base = share(jnp.int32(0), answers)
     _, base = lax.while_loop(
         lambda state: state[0] < turns[0],
         lambda state: (state[0] + 1, state[1] + share(state[0])),
         (jnp.int32(1), base),
     )
-    near_base = ring_small(base, Y_UP, Y_DOWN)
     answers = lax.all_to_all(answers, "walker", split_axis=0, concat_axis=0, tiled=True)
     change = simple(
         collect_kernel,
@@ -388,9 +408,10 @@
         target,
         answers.reshape(SERVERS * SLOTS, BLOCK),
         old_rows.reshape(ALL, BLOCK),
-        name="collect",
-    )
+    )
+    base, change = lax.optimization_barrier((base, change))
     near_change = ring_small(change, X_UP, X_DOWN)
+    near_base = ring_small(base, Y_UP, Y_DOWN)
     near_base, near_change = lax.optimization_barrier((near_base, near_change))
     change_pieces = ring_large(near_change, Y_UP, Y_DOWN)
     base_pieces = ring_large(near_base, X_UP, X_DOWN)

time: 117 us -> 108 us (0.923)
  waiting for transfers between devices: 50.4 us -> 40.5 us
    ppermute x16 -> x22, starting transfers between devices: 21.8 us -> 30.2 us  [send(): return lax.ppermute(x, 'col', pairs)]
    all_to_all x1 -> x0, starting transfers between devices: 7.17 us -> none  [share(): lax.all_to_all(picked, 'col', split_axis=0, concat_axis=0, tiled=True)]
    all_to_all x1 -> x0, waiting for transfers between devices: 5.78 us -> none  [share(): lax.all_to_all(picked, 'col', split_axis=0, concat_axis=0, tiled=True)]
    all_to_all x1, waiting for transfers between devices: 2.62 us -> 0.01 us  [local(): lax.all_to_all(answers, 'walker', split_axis=0, concat_axis=0, tiled=True)]
    ppermute x16 -> x22, waiting for transfers between devices: 39 us -> 36.6 us  [send(): return lax.ppermute(x, 'col', pairs)]
  transfers between devices with their start and end apart: 19 -> 24, of which waited for: 13 -> 15; matrix products, arithmetic and copies ran while one was open for 0% -> 0% of each run, Pallas kernels for 7% -> 4%
where the time goes in v1:
time: 108 us; the launch traced here: 107 us
  starting transfers between devices  42.4 us (39%)
  waiting for transfers between devices  40.5 us (38%)
  Pallas kernels  22.7 us (21%)
    ppermute x22, waiting for transfers between devices, send(): return lax.ppermute(x, 'col', pairs)  36.6 us
    ppermute x22, starting transfers between devices, send(): return lax.ppermute(x, 'col', pairs)  30.2 us
    pallas_call x1, Pallas kernels, local(): pl.pallas_call(update_kernel, in_specs=[VMEM] * 11, out_specs=ANY, out_sh...  12.5 us
    all_to_all x1, starting transfers between devices, local(): lax.all_to_all(sent.reshape(SERVERS, CAP, 128), 'walker', split_axis=0, c...  8.57 us
    pallas_call x4, Pallas kernels, simple(): pl.pallas_call(kernel, in_specs=specs or [VMEM] * len(args), out_specs=ou...  6.41 us
    all_to_all x1, waiting for transfers between devices, local(): lax.all_to_all(sent.reshape(SERVERS, CAP, 128), 'walker', split_axis=0, c...  3.94 us
    pallas_call x1, Pallas kernels, pick(): pl.pallas_call(pick_kernel, grid=(SIDE,), in_specs=[SMEM, pl.BlockSpec((1...  3.82 us
    all_to_all x1, starting transfers between devices, local(): lax.all_to_all(answers, 'walker', split_axis=0, concat_axis=0, tiled=True)  3.57 us
  transfers between devices with their start and end apart: 24, of which 15 were waited for; matrix products, arithmetic and copies ran while one was open for 0% of the time, Pallas kernels for 4%

profile of v1, /device:TPU:24, one launch (start us, length us, event | category | flops | bytes accessed | tf_op | source)
XLA Modules:
  0.0 107.4 jit_solution(5775478230360948349)
XLA Ops:
  0.0 2.6 %shard_map.82 = (f32[128,128]{1,0:T(8,128)}, s32[384,128]{1,0:T(8,128)}, s32[1,384]{1,0:T(1,128)S(1)}, s32[384,128]{1,0:T(8,128)S(1)}) custom-call(s32[6,1,64]{2,1,0:T(1,128)} %bitcast.92, s32[6,1,64]{2,1,0:T(1,128)} %bricks_ref.1, s32[6,1,64]{2,1,0:T(1,128)} %accept_ref.1, s32[6,1,64]{2,1,0:T(1,128)} %movers_ref.1, f32[3,6,1,64]{3,2,1,0:T(1,128)} %spots_ref.1), custom_call_target="tpu_custom_call" | custom-call | tf_op jit(solution)/shard_map/pallas_call | solution.py:213
  2.6 8.6 %all-to-all-start = ((f32[16,8,128]{2,1,0:T(8,128)}), f32[16,8,128]{2,1,0:T(8,128)S(1)}, u32[]{:S(2)}, u32[]{:S(2)}) async-start(f32[16,8,128]{2,1,0:T(8,128)} %bitcast.91), calls=%async_computation | async-start | bytes 131072 | tf_op jit(solution)/shard_map/all_to_all | solution.py:361
  11.2 3.8 %pick.2 = bf16[4,4,48,256]{3,2,1,0:T(8,128)(2,1)S(1)} custom-call(s32[1]{0:T(128)} %constant.2.clone.1.turn_ref, s32[1,384]{1,0:T(1,128)S(1)} %get-tuple-element.190.movers_ref, s32[384,128]{1,0:T(8,128)S(1)} %get-tuple-element.191.key_ref, f32[4096,256]{1,0:T(8,128)} %bitcast.84), custom_call_target="tpu_custom_call" | custom-call | flops 100000000 | bytes 5000000 | tf_op jit(solution)/shard_map/pick/pallas_call | solution.py:193
  15.1 3.9 %all-to-all-done = f32[16,8,128]{2,1,0:T(8,128)S(1)} async-done(((f32[16,8,128]{2,1,0:T(8,128)}), f32[16,8,128]{2,1,0:T(8,128)S(1)}, u32[]{:S(2)}, u32[]{:S(2)}) %all-to-all-start) | async-done | bytes 65568 | tf_op jit(solution)/shard_map/all_to_all | solution.py:361
  19.0 2.6 %shard_map.83 = (bf16[16,48,256]{2,1,0:T(8,128)(2,1)}, s32[1]{0:T(128)}) custom-call(f32[128,128]{1,0:T(8,128)S(1)} %bitcast.79, bf16[2048,256]{1,0:T(8,128)(2,1)S(1)} %bitcast.76), custom_call_target="tpu_custom_call" | custom-call | tf_op jit(solution)/shard_map/pallas_call | solution.py:213
  21.6 3.6 %all-to-all-start.1 = ((bf16[16,48,256]{2,1,0:T(8,128)(2,1)}), bf16[16,48,256]{2,1,0:T(8,128)(2,1)S(1)}, u32[]{:S(2)}, u32[]{:S(2)}) async-start(bf16[16,48,256]{2,1,0:T(8,128)(2,1)} %get-tuple-element.52), calls=%async_computation.1 | async-start | bytes 786432 | tf_op jit(solution)/shard_map/all_to_all | solution.py:404
  25.2 1.6 %collective-permute-start.6 = (bf16[4,48,256]{2,1,0:T(8,128)(2,1)S(1)}, bf16[4,48,256]{2,1,0:T(8,128)(2,1)S(1)}, u32[]{:S(2)}, u32[]{:S(2)}) collective-permute-start(bf16[4,48,256]{2,1,0:T(8,128)(2,1)S(1)} %get-tuple-element.96), channel_id=1, source_target_pairs={{0,1},{1,2},{2,3},{3,0},{4,5},{5,6},{6,7},{7,4},{8,9},{9,10},{10,1... | collective-permute-start | bytes 294920 | tf_op jit(solution)/shard_map/ppermute | solution.py:234
  26.8 1.8 %collective-permute-start.8 = (bf16[4,48,256]{2,1,0:T(8,128)(2,1)S(1)}, bf16[4,48,256]{2,1,0:T(8,128)(2,1)S(1)}, u32[]{:S(2)}, u32[]{:S(2)}) collective-permute-start(bf16[4,48,256]{2,1,0:T(8,128)(2,1)S(1)} %get-tuple-element.97), channel_id=1, source_target_pairs={{0,3},{1,0},{2,1},{3,2},{4,7},{5,4},{6,5},{7,6},{8,11},{9,8},{10,9... | collective-permute-start | bytes 294920 | tf_op jit(solution)/shard_map/ppermute | solution.py:234
  28.6 1.8 %collective-permute-start.7 = (bf16[4,48,256]{2,1,0:T(8,128)(2,1)S(1)}, bf16[4,48,256]{2,1,0:T(8,128)(2,1)S(1)}, u32[]{:S(2)}, u32[]{:S(2)}) collective-permute-start(bf16[4,48,256]{2,1,0:T(8,128)(2,1)S(1)} %get-tuple-element.98), channel_id=1, source_target_pairs={{0,2},{1,3},{2,0},{3,1},{4,6},{5,7},{6,4},{7,5},{8,10},{9,11},{10,... | collective-permute-start | bytes 294920 | tf_op jit(solution)/shard_map/ppermute | solution.py:234
  30.4 1.1 collective-permute-done.6
  31.5 1.5 %collective-permute-done.8 = bf16[4,48,256]{2,1,0:T(8,128)(2,1)S(1)} collective-permute-done((bf16[4,48,256]{2,1,0:T(8,128)(2,1)S(1)}, bf16[4,48,256]{2,1,0:T(8,128)(2,1)S(1)}, u32[]{:S(2)}, u32[]{:S(2)}) %collective-permute-start.8) | collective-permute-done | bytes 98336 | tf_op jit(solution)/shard_map/ppermute | solution.py:234
  33.0 1.7 %collective-permute-done.7 = bf16[4,48,256]{2,1,0:T(8,128)(2,1)S(1)} collective-permute-done((bf16[4,48,256]{2,1,0:T(8,128)(2,1)S(1)}, bf16[4,48,256]{2,1,0:T(8,128)(2,1)S(1)}, u32[]{:S(2)}, u32[]{:S(2)}) %collective-permute-start.7) | collective-permute-done | bytes 98336 | tf_op jit(solution)/shard_map/ppermute | solution.py:234
  35.1 2.7 %collective-permute-start.10 = (bf16[4,48,256]{2,1,0:T(8,128)(2,1)S(1)}, bf16[4,48,256]{2,1,0:T(8,128)(2,1)S(1)}, u32[]{:S(2)}, u32[]{:S(2)}) collective-permute-start(bf16[4,48,256]{2,1,0:T(8,128)(2,1)S(1)} %pad_maximum_fusion.8), channel_id=1, source_target_pairs={{0,8},{1,9},{2,10},{3,11},{4,12},{5,13},{6,14},{7,15},{8,0},{9,1},... | collective-permute-start | bytes 294920 | tf_op jit(solution)/shard_map/ppermute | solution.py:234
  37.9 1.7 %collective-permute-done.9 = bf16[4,48,256]{2,1,0:T(8,128)(2,1)S(1)} collective-permute-done((bf16[4,48,256]{2,1,0:T(8,128)(2,1)S(1)}, bf16[4,48,256]{2,1,0:T(8,128)(2,1)S(1)}, u32[]{:S(2)}, u32[]{:S(2)}) %collective-permute-start.9) | collective-permute-done | bytes 98336 | tf_op jit(solution)/shard_map/ppermute | solution.py:234
  39.5 2.7 %collective-permute-done.10 = bf16[4,48,256]{2,1,0:T(8,128)(2,1)S(1)} collective-permute-done((bf16[4,48,256]{2,1,0:T(8,128)(2,1)S(1)}, bf16[4,48,256]{2,1,0:T(8,128)(2,1)S(1)}, u32[]{:S(2)}, u32[]{:S(2)}) %collective-permute-start.10) | collective-permute-done | bytes 98336 | tf_op jit(solution)/shard_map/ppermute | solution.py:234
  42.2 1.4 %collective-permute-done.11 = bf16[4,48,256]{2,1,0:T(8,128)(2,1)S(1)} collective-permute-done((bf16[4,48,256]{2,1,0:T(8,128)(2,1)S(1)}, bf16[4,48,256]{2,1,0:T(8,128)(2,1)S(1)}, u32[]{:S(2)}, u32[]{:S(2)}) %collective-permute-start.11) | collective-permute-done | bytes 98336 | tf_op jit(solution)/shard_map/ppermute | solution.py:234
  45.8 3.2 %collective-permute-start.12 = (bf16[256,384]{1,0:T(8,128)(2,1)S(1)}, bf16[256,384]{1,0:T(8,128)(2,1)S(1)}, u32[]{:S(2)}, u32[]{:S(2)}) collective-permute-start(bf16[256,384]{1,0:T(8,128)(2,1)S(1)} %get-tuple-element.57), channel_id=1, source_target_pairs={{0,4},{1,5},{2,6},{3,7},{4,8},{5,9},{6,10},{7,11},{8,12},{9,13},{1... | collective-permute-start | bytes 589832 | tf_op jit(solution)/shard_map/ppermute | solution.py:234
  49.0 1.9 %collective-permute-start.17 = (bf16[384,256]{1,0:T(8,128)(2,1)S(1)}, bf16[384,256]{1,0:T(8,128)(2,1)S(1)}, u32[]{:S(2)}, u32[]{:S(2)}) collective-permute-start(bf16[384,256]{1,0:T(8,128)(2,1)S(1)} %shard_map.85), channel_id=1, source_target_pairs={{0,3},{1,0},{2,1},{3,2},{4,7},{5,4},{6,5},{7,6},{8,11},{9,8},{10,9... | collective-permute-start | bytes 589832 | tf_op jit(solution)/shard_map/ppermute | solution.py:234
  51.0 1.6 %collective-permute-done.13 = bf16[256,384]{1,0:T(8,128)(2,1)S(1)} collective-permute-done((bf16[256,384]{1,0:T(8,128)(2,1)S(1)}, bf16[256,384]{1,0:T(8,128)(2,1)S(1)}, u32[]{:S(2)}, u32[]{:S(2)}) %collective-permute-start.13) | collective-permute-done | bytes 196640 | tf_op jit(solution)/shard_map/ppermute | solution.py:234
  52.8 3.3 %collective-permute-start.14 = (bf16[128,384]{1,0:T(8,128)(2,1)S(1)}, bf16[128,384]{1,0:T(8,128)(2,1)S(1)}, u32[]{:S(2)}, u32[]{:S(2)}) collective-permute-start(bf16[128,384]{1,0:T(8,128)(2,1)S(1)} %slice.234), channel_id=1, source_target_pairs={{0,4},{1,5},{2,6},{3,7},{4,8},{5,9},{6,10},{7,11},{8,12},{9,13},{1... | collective-permute-start | bytes 294920 | tf_op jit(solution)/shard_map/ppermute | solution.py:234
  56.1 2.0 %collective-permute-start.19 = (bf16[192,256]{1,0:T(8,128)(2,1)S(1)}, bf16[192,256]{1,0:T(8,128)(2,1)S(1)}, u32[]{:S(2)}, u32[]{:S(2)}) collective-permute-start(bf16[192,256]{1,0:T(8,128)(2,1)S(1)} %slice.237), channel_id=1, source_target_pairs={{0,3},{1,0},{2,1},{3,2},{4,7},{5,4},{6,5},{7,6},{8,11},{9,8},{10,9... | collective-permute-start | bytes 294920 | tf_op jit(solution)/shard_map/ppermute | solution.py:234
  58.7 2.1 %collective-permute-done.19 = bf16[192,256]{1,0:T(8,128)(2,1)S(1)} collective-permute-done((bf16[192,256]{1,0:T(8,128)(2,1)S(1)}, bf16[192,256]{1,0:T(8,128)(2,1)S(1)}, u32[]{:S(2)}, u32[]{:S(2)}) %collective-permute-start.19) | collective-permute-done | bytes 98336 | tf_op jit(solution)/shard_map/ppermute | solution.py:234
  60.8 3.2 %collective-permute-done.18 = bf16[192,256]{1,0:T(8,128)(2,1)S(1)} collective-permute-done((bf16[192,256]{1,0:T(8,128)(2,1)S(1)}, bf16[192,256]{1,0:T(8,128)(2,1)S(1)}, u32[]{:S(2)}, u32[]{:S(2)}) %collective-permute-start.18) | collective-permute-done | bytes 98336 | tf_op jit(solution)/shard_map/ppermute | solution.py:234
  64.4 3.2 %collective-permute-start.20 = (bf16[4,384,256]{2,1,0:T(8,128)(2,1)S(1)}, bf16[4,384,256]{2,1,0:T(8,128)(2,1)S(1)}, u32[]{:S(2)}, u32[]{:S(2)}) collective-permute-start(bf16[4,384,256]{2,1,0:T(8,128)(2,1)S(1)} %pad_maximum_fusion.5.refs_0_), channel_id=1, source_target_pairs={{0,4},{1,5},{2,6},{3,7},{4,8},{5,9},{6,10},{7,11},{8,12},{9,13},{1... | collective-permute-start | bytes 2359304 | tf_op jit(solution)/shard_map/ppermute | solution.py:234
  67.7 2.0 %collective-permute-start.24 = (bf16[4,256,384]{2,1,0:T(8,128)(2,1)S(1)}, bf16[4,256,384]{2,1,0:T(8,128)(2,1)S(1)}, u32[]{:S(2)}, u32[]{:S(2)}) collective-permute-start(bf16[4,256,384]{2,1,0:T(8,128)(2,1)S(1)} %pad_maximum_fusion.4.refs_5_), channel_id=1, source_target_pairs={{0,1},{1,2},{2,3},{3,0},{4,5},{5,6},{6,7},{7,4},{8,9},{9,10},{10,1... | collective-permute-start | bytes 2359304 | tf_op jit(solution)/shard_map/ppermute | solution.py:234
  69.7 12.3 %collective-permute-done.21.refs_2_ = bf16[4,384,256]{2,1,0:T(8,128)(2,1)S(1)} collective-permute-done((bf16[4,384,256]{2,1,0:T(8,128)(2,1)S(1)}, bf16[4,384,256]{2,1,0:T(8,128)(2,1)S(1)}, u32[]{:S(2)}, u32[]{:S(2)}) %collective-permute-start.21) | collective-permute-done | bytes 786464 | tf_op jit(solution)/shard_map/ppermute | solution.py:234
  82.2 3.3 %collective-permute-start.22 = (bf16[2,384,256]{2,1,0:T(8,128)(2,1)S(1)}, bf16[2,384,256]{2,1,0:T(8,128)(2,1)S(1)}, u32[]{:S(2)}, u32[]{:S(2)}) collective-permute-start(bf16[2,384,256]{2,1,0:T(8,128)(2,1)S(1)} %slice.238), channel_id=1, source_target_pairs={{0,4},{1,5},{2,6},{3,7},{4,8},{5,9},{6,10},{7,11},{8,12},{9,13},{1... | collective-permute-start | bytes 1179656 | tf_op jit(solution)/shard_map/ppermute | solution.py:234
  85.7 2.1 %collective-permute-start.26 = (bf16[2,256,384]{2,1,0:T(8,128)(2,1)S(1)}, bf16[2,256,384]{2,1,0:T(8,128)(2,1)S(1)}, u32[]{:S(2)}, u32[]{:S(2)}) collective-permute-start(bf16[2,256,384]{2,1,0:T(8,128)(2,1)S(1)} %slice.240), channel_id=1, source_target_pairs={{0,1},{1,2},{2,3},{3,0},{4,5},{5,6},{6,7},{7,4},{8,9},{9,10},{10,1... | collective-permute-start | bytes 1179656 | tf_op jit(solution)/shard_map/ppermute | solution.py:234
  87.8 3.4 %collective-permute-done.23.refs_4_ = bf16[2,384,256]{2,1,0:T(8,128)(2,1)S(1)} collective-permute-done((bf16[2,384,256]{2,1,0:T(8,128)(2,1)S(1)}, bf16[2,384,256]{2,1,0:T(8,128)(2,1)S(1)}, u32[]{:S(2)}, u32[]{:S(2)}) %collective-permute-start.23) | collective-permute-done | bytes 393248 | tf_op jit(solution)/shard_map/ppermute | solution.py:234
  91.1 2.3 %collective-permute-done.27.refs_9_ = bf16[2,256,384]{2,1,0:T(8,128)(2,1)S(1)} collective-permute-done((bf16[2,256,384]{2,1,0:T(8,128)(2,1)S(1)}, bf16[2,256,384]{2,1,0:T(8,128)(2,1)S(1)}, u32[]{:S(2)}, u32[]{:S(2)}) %collective-permute-start.27) | collective-permute-done | bytes 393248 | tf_op jit(solution)/shard_map/ppermute | solution.py:234
  93.4 1.4 %collective-permute-done.26.refs_8_ = bf16[2,256,384]{2,1,0:T(8,128)(2,1)S(1)} collective-permute-done((bf16[2,256,384]{2,1,0:T(8,128)(2,1)S(1)}, bf16[2,256,384]{2,1,0:T(8,128)(2,1)S(1)}, u32[]{:S(2)}, u32[]{:S(2)}) %collective-permute-start.26) | collective-permute-done | bytes 393248 | tf_op jit(solution)/shard_map/ppermute | solution.py:234
  94.7 12.5 %update.1 = f32[4096,256]{1,0:T(8,128)} custom-call(bf16[4,384,256]{2,1,0:T(8,128)(2,1)S(1)} %pad_maximum_fusion.5.refs_0_, bf16[4,384,256]{2,1,0:T(8,128)(2,1)S(1)} %collective-permute-done.20.refs_1_, bf16[4,384,256]{2,1,0:T(8,128)(2,1)S(1)} %collective-permute-done.21.refs_2_, bf16[2,384,256]{2,1,0:T(8,128)(2,1)S(1)} %collective-permute-done.22.refs_3_, ...), custom_call_target="tpu_custom_call" | custom-call | tf_op jit(solution)/shard_map/update/pallas_call | solution.py:418
  (52 shorter events, 4.1 us)
Async XLA Ops:
  0.0 19.0 %copy-start = (bf16[32,64,256]{2,1,0:T(8,128)(2,1)S(1)}, bf16[32,64,256]{2,1,0:T(8,128)(2,1)}, u32[]{:S(2)}) copy-start(bf16[32,64,256]{2,1,0:T(8,128)(2,1)} %param.11) | copy-start | bytes 3145732
  2.6 16.4 %all-to-all-start = ((f32[16,8,128]{2,1,0:T(8,128)}), f32[16,8,128]{2,1,0:T(8,128)S(1)}, u32[]{:S(2)}, u32[]{:S(2)}) async-start(f32[16,8,128]{2,1,0:T(8,128)} %bitcast.91), calls=%async_computation | async-start | bytes 131072 | tf_op jit(solution)/shard_map/all_to_all | solution.py:361
  11.2 33.3 %copy-start.1 = (bf16[6,1,64,256]{3,2,1,0:T(8,128)(2,1)S(1)}, bf16[6,1,64,256]{3,2,1,0:T(8,128)(2,1)}, u32[]{:S(2)}) copy-start(bf16[6,1,64,256]{3,2,1,0:T(8,128)(2,1)} %param.17) | copy-start | bytes 589828
  11.2 33.3 %copy-start.2 = (s32[384,128]{1,0:T(8,128)S(1)}, s32[384,128]{1,0:T(8,128)}, u32[]{:S(2)}) copy-start(s32[384,128]{1,0:T(8,128)} %get-tuple-element.56.target_ref) | copy-start | bytes 589828
  21.6 22.9 %all-to-all-start.1 = ((bf16[16,48,256]{2,1,0:T(8,128)(2,1)}), bf16[16,48,256]{2,1,0:T(8,128)(2,1)S(1)}, u32[]{:S(2)}, u32[]{:S(2)}) async-start(bf16[16,48,256]{2,1,0:T(8,128)(2,1)} %get-tuple-element.52), calls=%async_computation.1 | async-start | bytes 786432 | tf_op jit(solution)/shard_map/all_to_all | solution.py:404
  25.2 6.3 %collective-permute-start.6 = (bf16[4,48,256]{2,1,0:T(8,128)(2,1)S(1)}, bf16[4,48,256]{2,1,0:T(8,128)(2,1)S(1)}, u32[]{:S(2)}, u32[]{:S(2)}) collective-permute-start(bf16[4,48,256]{2,1,0:T(8,128)(2,1)S(1)} %get-tuple-element.96), channel_id=1, source_target_pairs={{0,1},{1,2},{2,3},{3,0},{4,5},{5,6},{6,7},{7,4},{8,9},{9,10},{10,1... | collective-permute-start | bytes 294920 | tf_op jit(solution)/shard_map/ppermute | solution.py:234
  26.8 6.2 %collective-permute-start.8 = (bf16[4,48,256]{2,1,0:T(8,128)(2,1)S(1)}, bf16[4,48,256]{2,1,0:T(8,128)(2,1)S(1)}, u32[]{:S(2)}, u32[]{:S(2)}) collective-permute-start(bf16[4,48,256]{2,1,0:T(8,128)(2,1)S(1)} %get-tuple-element.97), channel_id=1, source_target_pairs={{0,3},{1,0},{2,1},{3,2},{4,7},{5,4},{6,5},{7,6},{8,11},{9,8},{10,9... | collective-permute-start | bytes 294920 | tf_op jit(solution)/shard_map/ppermute | solution.py:234
  28.6 6.1 %collective-permute-start.7 = (bf16[4,48,256]{2,1,0:T(8,128)(2,1)S(1)}, bf16[4,48,256]{2,1,0:T(8,128)(2,1)S(1)}, u32[]{:S(2)}, u32[]{:S(2)}) collective-permute-start(bf16[4,48,256]{2,1,0:T(8,128)(2,1)S(1)} %get-tuple-element.98), channel_id=1, source_target_pairs={{0,2},{1,3},{2,0},{3,1},{4,6},{5,7},{6,4},{7,5},{8,10},{9,11},{10,... | collective-permute-start | bytes 294920 | tf_op jit(solution)/shard_map/ppermute | solution.py:234
  34.7 4.8 %collective-permute-start.9 = (bf16[4,48,256]{2,1,0:T(8,128)(2,1)S(1)}, bf16[4,48,256]{2,1,0:T(8,128)(2,1)S(1)}, u32[]{:S(2)}, u32[]{:S(2)}) collective-permute-start(bf16[4,48,256]{2,1,0:T(8,128)(2,1)S(1)} %pad_maximum_fusion.7), channel_id=1, source_target_pairs={{0,4},{1,5},{2,6},{3,7},{4,8},{5,9},{6,10},{7,11},{8,12},{9,13},{1... | collective-permute-start | bytes 294920 | tf_op jit(solution)/shard_map/ppermute | solution.py:234
  35.1 7.1 %collective-permute-start.10 = (bf16[4,48,256]{2,1,0:T(8,128)(2,1)S(1)}, bf16[4,48,256]{2,1,0:T(8,128)(2,1)S(1)}, u32[]{:S(2)}, u32[]{:S(2)}) collective-permute-start(bf16[4,48,256]{2,1,0:T(8,128)(2,1)S(1)} %pad_maximum_fusion.8), channel_id=1, source_target_pairs={{0,8},{1,9},{2,10},{3,11},{4,12},{5,13},{6,14},{7,15},{8,0},{9,1},... | collective-permute-start | bytes 294920 | tf_op jit(solution)/shard_map/ppermute | solution.py:234
  37.8 5.9 %collective-permute-start.11 = (bf16[4,48,256]{2,1,0:T(8,128)(2,1)S(1)}, bf16[4,48,256]{2,1,0:T(8,128)(2,1)S(1)}, u32[]{:S(2)}, u32[]{:S(2)}) collective-permute-start(bf16[4,48,256]{2,1,0:T(8,128)(2,1)S(1)} %pad_maximum_fusion.9), channel_id=1, source_target_pairs={{0,12},{1,13},{2,14},{3,15},{4,0},{5,1},{6,2},{7,3},{8,4},{9,5},{1... | collective-permute-start | bytes 294920 | tf_op jit(solution)/shard_map/ppermute | solution.py:234
  45.7 49.1 %copy-start.3 = (f32[4096,256]{1,0:T(8,128)S(1)}, f32[4096,256]{1,0:T(8,128)}, u32[]{:S(2)}) copy-start(f32[4096,256]{1,0:T(8,128)} %get-tuple-element.230) | copy-start | bytes 12582916
  45.7 7.0 %collective-permute-start.13 = (bf16[256,384]{1,0:T(8,128)(2,1)S(1)}, bf16[256,384]{1,0:T(8,128)(2,1)S(1)}, u32[]{:S(2)}, u32[]{:S(2)}) collective-permute-start(bf16[256,384]{1,0:T(8,128)(2,1)S(1)} %get-tuple-element.57), channel_id=1, source_target_pairs={{0,12},{1,13},{2,14},{3,15},{4,0},{5,1},{6,2},{7,3},{8,4},{9,5},{1... | collective-permute-start | bytes 589832 | tf_op jit(solution)/shard_map/ppermute | solution.py:234
  45.8 7.0 %collective-permute-start.12 = (bf16[256,384]{1,0:T(8,128)(2,1)S(1)}, bf16[256,384]{1,0:T(8,128)(2,1)S(1)}, u32[]{:S(2)}, u32[]{:S(2)}) collective-permute-start(bf16[256,384]{1,0:T(8,128)(2,1)S(1)} %get-tuple-element.57), channel_id=1, source_target_pairs={{0,4},{1,5},{2,6},{3,7},{4,8},{5,9},{6,10},{7,11},{8,12},{9,13},{1... | collective-permute-start | bytes 589832 | tf_op jit(solution)/shard_map/ppermute | solution.py:234
  49.0 7.1 %collective-permute-start.17 = (bf16[384,256]{1,0:T(8,128)(2,1)S(1)}, bf16[384,256]{1,0:T(8,128)(2,1)S(1)}, u32[]{:S(2)}, u32[]{:S(2)}) collective-permute-start(bf16[384,256]{1,0:T(8,128)(2,1)S(1)} %shard_map.85), channel_id=1, source_target_pairs={{0,3},{1,0},{2,1},{3,2},{4,7},{5,4},{6,5},{7,6},{8,11},{9,8},{10,9... | collective-permute-start | bytes 589832 | tf_op jit(solution)/shard_map/ppermute | solution.py:234
  50.9 7.2 %collective-permute-start.16 = (bf16[384,256]{1,0:T(8,128)(2,1)S(1)}, bf16[384,256]{1,0:T(8,128)(2,1)S(1)}, u32[]{:S(2)}, u32[]{:S(2)}) collective-permute-start(bf16[384,256]{1,0:T(8,128)(2,1)S(1)} %shard_map.85), channel_id=1, source_target_pairs={{0,1},{1,2},{2,3},{3,0},{4,5},{5,6},{6,7},{7,4},{8,9},{9,10},{10,1... | collective-permute-start | bytes 589832 | tf_op jit(solution)/shard_map/ppermute | solution.py:234
  52.6 5.9 %collective-permute-start.15 = (bf16[128,384]{1,0:T(8,128)(2,1)S(1)}, bf16[128,384]{1,0:T(8,128)(2,1)S(1)}, u32[]{:S(2)}, u32[]{:S(2)}) collective-permute-start(bf16[128,384]{1,0:T(8,128)(2,1)S(1)} %slice.235), channel_id=1, source_target_pairs={{0,12},{1,13},{2,14},{3,15},{4,0},{5,1},{6,2},{7,3},{8,4},{9,5},{1... | collective-permute-start | bytes 294920 | tf_op jit(solution)/shard_map/ppermute | solution.py:234
  52.8 5.8 %collective-permute-start.14 = (bf16[128,384]{1,0:T(8,128)(2,1)S(1)}, bf16[128,384]{1,0:T(8,128)(2,1)S(1)}, u32[]{:S(2)}, u32[]{:S(2)}) collective-permute-start(bf16[128,384]{1,0:T(8,128)(2,1)S(1)} %slice.234), channel_id=1, source_target_pairs={{0,4},{1,5},{2,6},{3,7},{4,8},{5,9},{6,10},{7,11},{8,12},{9,13},{1... | collective-permute-start | bytes 294920 | tf_op jit(solution)/shard_map/ppermute | solution.py:234
  56.1 4.7 %collective-permute-start.19 = (bf16[192,256]{1,0:T(8,128)(2,1)S(1)}, bf16[192,256]{1,0:T(8,128)(2,1)S(1)}, u32[]{:S(2)}, u32[]{:S(2)}) collective-permute-start(bf16[192,256]{1,0:T(8,128)(2,1)S(1)} %slice.237), channel_id=1, source_target_pairs={{0,3},{1,0},{2,1},{3,2},{4,7},{5,4},{6,5},{7,6},{8,11},{9,8},{10,9... | collective-permute-start | bytes 294920 | tf_op jit(solution)/shard_map/ppermute | solution.py:234
  58.1 5.9 %collective-permute-start.18 = (bf16[192,256]{1,0:T(8,128)(2,1)S(1)}, bf16[192,256]{1,0:T(8,128)(2,1)S(1)}, u32[]{:S(2)}, u32[]{:S(2)}) collective-permute-start(bf16[192,256]{1,0:T(8,128)(2,1)S(1)} %slice.236), channel_id=1, source_target_pairs={{0,1},{1,2},{2,3},{3,0},{4,5},{5,6},{6,7},{7,4},{8,9},{9,10},{10,1... | collective-permute-start | bytes 294920 | tf_op jit(solution)/shard_map/ppermute | solution.py:234
  64.1 17.9 %collective-permute-start.21 = (bf16[4,384,256]{2,1,0:T(8,128)(2,1)S(1)}, bf16[4,384,256]{2,1,0:T(8,128)(2,1)S(1)}, u32[]{:S(2)}, u32[]{:S(2)}) collective-permute-start(bf16[4,384,256]{2,1,0:T(8,128)(2,1)S(1)} %pad_maximum_fusion.5.refs_0_), channel_id=1, source_target_pairs={{0,12},{1,13},{2,14},{3,15},{4,0},{5,1},{6,2},{7,3},{8,4},{9,5},{1... | collective-permute-start | bytes 2359304 | tf_op jit(solution)/shard_map/ppermute | solution.py:234
  64.4 17.7 %collective-permute-start.20 = (bf16[4,384,256]{2,1,0:T(8,128)(2,1)S(1)}, bf16[4,384,256]{2,1,0:T(8,128)(2,1)S(1)}, u32[]{:S(2)}, u32[]{:S(2)}) collective-permute-start(bf16[4,384,256]{2,1,0:T(8,128)(2,1)S(1)} %pad_maximum_fusion.5.refs_0_), channel_id=1, source_target_pairs={{0,4},{1,5},{2,6},{3,7},{4,8},{5,9},{6,10},{7,11},{8,12},{9,13},{1... | collective-permute-start | bytes 2359304 | tf_op jit(solution)/shard_map/ppermute | solution.py:234
  67.7 17.8 %collective-permute-start.25 = (bf16[4,256,384]{2,1,0:T(8,128)(2,1)S(1)}, bf16[4,256,384]{2,1,0:T(8,128)(2,1)S(1)}, u32[]{:S(2)}, u32[]{:S(2)}) collective-permute-start(bf16[4,256,384]{2,1,0:T(8,128)(2,1)S(1)} %pad_maximum_fusion.4.refs_5_), channel_id=1, source_target_pairs={{0,3},{1,0},{2,1},{3,2},{4,7},{5,4},{6,5},{7,6},{8,11},{9,8},{10,9... | collective-permute-start | bytes 2359304 | tf_op jit(solution)/shard_map/ppermute | solution.py:234
  67.7 18.0 %collective-permute-start.24 = (bf16[4,256,384]{2,1,0:T(8,128)(2,1)S(1)}, bf16[4,256,384]{2,1,0:T(8,128)(2,1)S(1)}, u32[]{:S(2)}, u32[]{:S(2)}) collective-permute-start(bf16[4,256,384]{2,1,0:T(8,128)(2,1)S(1)} %pad_maximum_fusion.4.refs_5_), channel_id=1, source_target_pairs={{0,1},{1,2},{2,3},{3,0},{4,5},{5,6},{6,7},{7,4},{8,9},{9,10},{10,1... | collective-permute-start | bytes 2359304 | tf_op jit(solution)/shard_map/ppermute | solution.py:234
  82.0 9.1 %collective-permute-start.23 = (bf16[2,384,256]{2,1,0:T(8,128)(2,1)S(1)}, bf16[2,384,256]{2,1,0:T(8,128)(2,1)S(1)}, u32[]{:S(2)}, u32[]{:S(2)}) collective-permute-start(bf16[2,384,256]{2,1,0:T(8,128)(2,1)S(1)} %slice.239), channel_id=1, source_target_pairs={{0,12},{1,13},{2,14},{3,15},{4,0},{5,1},{6,2},{7,3},{8,4},{9,5},{1... | collective-permute-start | bytes 1179656 | tf_op jit(solution)/shard_map/ppermute | solution.py:234
  82.2 8.9 %collective-permute-start.22 = (bf16[2,384,256]{2,1,0:T(8,128)(2,1)S(1)}, bf16[2,384,256]{2,1,0:T(8,128)(2,1)S(1)}, u32[]{:S(2)}, u32[]{:S(2)}) collective-permute-start(bf16[2,384,256]{2,1,0:T(8,128)(2,1)S(1)} %slice.238), channel_id=1, source_target_pairs={{0,4},{1,5},{2,6},{3,7},{4,8},{5,9},{6,10},{7,11},{8,12},{9,13},{1... | collective-permute-start | bytes 1179656 | tf_op jit(solution)/shard_map/ppermute | solution.py:234
  85.5 7.9 %collective-permute-start.27 = (bf16[2,256,384]{2,1,0:T(8,128)(2,1)S(1)}, bf16[2,256,384]{2,1,0:T(8,128)(2,1)S(1)}, u32[]{:S(2)}, u32[]{:S(2)}) collective-permute-start(bf16[2,256,384]{2,1,0:T(8,128)(2,1)S(1)} %slice.241), channel_id=1, source_target_pairs={{0,3},{1,0},{2,1},{3,2},{4,7},{5,4},{6,5},{7,6},{8,11},{9,8},{10,9... | collective-permute-start | bytes 1179656 | tf_op jit(solution)/shard_map/ppermute | solution.py:234
  85.7 9.1 %collective-permute-start.26 = (bf16[2,256,384]{2,1,0:T(8,128)(2,1)S(1)}, bf16[2,256,384]{2,1,0:T(8,128)(2,1)S(1)}, u32[]{:S(2)}, u32[]{:S(2)}) collective-permute-start(bf16[2,256,384]{2,1,0:T(8,128)(2,1)S(1)} %slice.240), channel_id=1, source_target_pairs={{0,1},{1,2},{2,3},{3,0},{4,5},{5,6},{6,7},{7,4},{8,9},{9,10},{10,1... | collective-permute-start | bytes 1179656 | tf_op jit(solution)/shard_map/ppermute | solution.py:234

commit v2 on v1

--- a/solution.py
+++ b/solution.py
@@ -376,10 +376,13 @@
             if step:
                 block = send(block, shift(step, 0))
             down.append(block.reshape(SIDE * SHARE, BLOCK))
+        return down
+
+    def place(turn, down):
         return simple(
             place_kernel,
             jax.ShapeDtypeStruct((BLOCK, ALL), bf16),
-            turn,
+            turn.reshape(1),
             key,
             *down,
             specs=[SMEM] + [VMEM] * (1 + SIDE),
@@ -395,12 +398,7 @@
         table.reshape(-1, BLOCK),
         outs=[VMEM, SMEM],
     )
-    base = share(jnp.int32(0), answers)
-    _, base = lax.while_loop(
-        lambda state: state[0] < turns[0],
-        lambda state: (state[0] + 1, state[1] + share(state[0])),
-        (jnp.int32(1), base),
-    )
+    shares = share(jnp.int32(0), answers)
     answers = lax.all_to_all(answers, "walker", split_axis=0, concat_axis=0, tiled=True)
     change = simple(
         collect_kernel,
@@ -409,8 +407,14 @@
         answers.reshape(SERVERS * SLOTS, BLOCK),
         old_rows.reshape(ALL, BLOCK),
     )
-    base, change = lax.optimization_barrier((base, change))
+    shares, _ = lax.optimization_barrier((shares, change))
     near_change = ring_small(change, X_UP, X_DOWN)
+    base = place(jnp.int32(0), shares)
+    _, base = lax.while_loop(
+        lambda state: state[0] < turns[0],
+        lambda state: (state[0] + 1, state[1] + place(state[0], share(state[0]))),
+        (jnp.int32(1), base),
+    )
     near_base = ring_small(base, Y_UP, Y_DOWN)
     near_base, near_change = lax.optimization_barrier((near_base, near_change))
     change_pieces = ring_large(near_change, Y_UP, Y_DOWN)

time: 108 us -> 106 us (0.981)
  waiting for transfers between devices: 40.5 us -> 37.6 us
    ppermute x22, waiting for transfers between devices: 36.6 us -> 32.9 us  [send(): return lax.ppermute(x, 'col', pairs)]
  transfers between devices with their start and end apart: 24 -> 24, of which waited for: 15 -> 15; matrix products, arithmetic and copies ran while one was open for 0% -> 0% of each run, Pallas kernels for 4% -> 5%
where the time goes in v2:
time: 106 us; the launch traced here: 105 us
  starting transfers between devices  43.2 us (41%)
  waiting for transfers between devices  37.6 us (35%)
  Pallas kernels  22.7 us (21%)
    ppermute x22, waiting for transfers between devices, send(): return lax.ppermute(x, 'col', pairs)  32.9 us
    ppermute x22, starting transfers between devices, send(): return lax.ppermute(x, 'col', pairs)  31.1 us
    pallas_call x1, Pallas kernels, local(): pl.pallas_call(update_kernel, in_specs=[VMEM] * 11, out_specs=ANY, out_sh...  12.5 us
    all_to_all x1, starting transfers between devices, local(): lax.all_to_all(sent.reshape(SERVERS, CAP, 128), 'walker', split_axis=0, c...  8.57 us
    pallas_call x4, Pallas kernels, simple(): pl.pallas_call(kernel, in_specs=specs or [VMEM] * len(args), out_specs=ou...  6.41 us
    all_to_all x1, waiting for transfers between devices, local(): lax.all_to_all(sent.reshape(SERVERS, CAP, 128), 'walker', split_axis=0, c...  3.94 us
    pallas_call x1, Pallas kernels, pick(): pl.pallas_call(pick_kernel, grid=(SIDE,), in_specs=[SMEM, pl.BlockSpec((1...  3.82 us
    all_to_all x1, starting transfers between devices, local(): lax.all_to_all(answers, 'walker', split_axis=0, concat_axis=0, tiled=True)  3.57 us
  transfers between devices with their start and end apart: 24, of which 15 were waited for; matrix products, arithmetic and copies ran while one was open for 0% of the time, Pallas kernels for 5%

profile of v2, /device:TPU:24, one launch (start us, length us, event | category | flops | bytes accessed | tf_op | source)
XLA Modules:
  0.0 105.2 jit_solution(7818509799143570387)
XLA Ops:
  0.0 2.6 %shard_map.82 = (f32[128,128]{1,0:T(8,128)}, s32[384,128]{1,0:T(8,128)}, s32[1,384]{1,0:T(1,128)S(1)}, s32[384,128]{1,0:T(8,128)S(1)}) custom-call(s32[6,1,64]{2,1,0:T(1,128)} %bitcast.92, s32[6,1,64]{2,1,0:T(1,128)} %bricks_ref.1, s32[6,1,64]{2,1,0:T(1,128)} %accept_ref.1, s32[6,1,64]{2,1,0:T(1,128)} %movers_ref.1, f32[3,6,1,64]{3,2,1,0:T(1,128)} %spots_ref.1), custom_call_target="tpu_custom_call" | custom-call | tf_op jit(solution)/shard_map/pallas_call | solution.py:213
  2.6 8.6 %all-to-all-start = ((f32[16,8,128]{2,1,0:T(8,128)}), f32[16,8,128]{2,1,0:T(8,128)S(1)}, u32[]{:S(2)}, u32[]{:S(2)}) async-start(f32[16,8,128]{2,1,0:T(8,128)} %bitcast.91), calls=%async_computation | async-start | bytes 131072 | tf_op jit(solution)/shard_map/all_to_all | solution.py:361
  11.2 3.8 %pick.2 = bf16[4,4,48,256]{3,2,1,0:T(8,128)(2,1)S(1)} custom-call(s32[1]{0:T(128)} %constant.2.clone.1.turn_ref, s32[1,384]{1,0:T(1,128)S(1)} %get-tuple-element.194.movers_ref, s32[384,128]{1,0:T(8,128)S(1)} %get-tuple-element.195.key_ref, f32[4096,256]{1,0:T(8,128)} %bitcast.84), custom_call_target="tpu_custom_call" | custom-call | flops 100000000 | bytes 5000000 | tf_op jit(solution)/shard_map/pick/pallas_call | solution.py:193
  15.1 3.9 %all-to-all-done = f32[16,8,128]{2,1,0:T(8,128)S(1)} async-done(((f32[16,8,128]{2,1,0:T(8,128)}), f32[16,8,128]{2,1,0:T(8,128)S(1)}, u32[]{:S(2)}, u32[]{:S(2)}) %all-to-all-start) | async-done | bytes 65568 | tf_op jit(solution)/shard_map/all_to_all | solution.py:361
  19.0 2.6 %shard_map.83 = (bf16[16,48,256]{2,1,0:T(8,128)(2,1)}, s32[1]{0:T(128)}) custom-call(f32[128,128]{1,0:T(8,128)S(1)} %bitcast.79, bf16[2048,256]{1,0:T(8,128)(2,1)S(1)} %bitcast.76), custom_call_target="tpu_custom_call" | custom-call | tf_op jit(solution)/shard_map/pallas_call | solution.py:213
  21.6 3.6 %all-to-all-start.1 = ((bf16[16,48,256]{2,1,0:T(8,128)(2,1)}), bf16[16,48,256]{2,1,0:T(8,128)(2,1)S(1)}, u32[]{:S(2)}, u32[]{:S(2)}) async-start(bf16[16,48,256]{2,1,0:T(8,128)(2,1)} %get-tuple-element.54), calls=%async_computation.1 | async-start | bytes 786432 | tf_op jit(solution)/shard_map/all_to_all | solution.py:402
  25.2 1.6 %collective-permute-start.6 = (bf16[4,48,256]{2,1,0:T(8,128)(2,1)S(1)}, bf16[4,48,256]{2,1,0:T(8,128)(2,1)S(1)}, u32[]{:S(2)}, u32[]{:S(2)}) collective-permute-start(bf16[4,48,256]{2,1,0:T(8,128)(2,1)S(1)} %get-tuple-element.100), channel_id=1, source_target_pairs={{0,1},{1,2},{2,3},{3,0},{4,5},{5,6},{6,7},{7,4},{8,9},{9,10},{10,1... | collective-permute-start | bytes 294920 | tf_op jit(solution)/shard_map/ppermute | solution.py:234
  26.8 1.8 %collective-permute-start.8 = (bf16[4,48,256]{2,1,0:T(8,128)(2,1)S(1)}, bf16[4,48,256]{2,1,0:T(8,128)(2,1)S(1)}, u32[]{:S(2)}, u32[]{:S(2)}) collective-permute-start(bf16[4,48,256]{2,1,0:T(8,128)(2,1)S(1)} %get-tuple-element.101), channel_id=1, source_target_pairs={{0,3},{1,0},{2,1},{3,2},{4,7},{5,4},{6,5},{7,6},{8,11},{9,8},{10,9... | collective-permute-start | bytes 294920 | tf_op jit(solution)/shard_map/ppermute | solution.py:234
  28.6 1.8 %collective-permute-start.7 = (bf16[4,48,256]{2,1,0:T(8,128)(2,1)S(1)}, bf16[4,48,256]{2,1,0:T(8,128)(2,1)S(1)}, u32[]{:S(2)}, u32[]{:S(2)}) collective-permute-start(bf16[4,48,256]{2,1,0:T(8,128)(2,1)S(1)} %get-tuple-element.102), channel_id=1, source_target_pairs={{0,2},{1,3},{2,0},{3,1},{4,6},{5,7},{6,4},{7,5},{8,10},{9,11},{10,... | collective-permute-start | bytes 294920 | tf_op jit(solution)/shard_map/ppermute | solution.py:234
  30.4 1.1 %collective-permute-done.6 = bf16[4,48,256]{2,1,0:T(8,128)(2,1)S(1)} collective-permute-done((bf16[4,48,256]{2,1,0:T(8,128)(2,1)S(1)}, bf16[4,48,256]{2,1,0:T(8,128)(2,1)S(1)}, u32[]{:S(2)}, u32[]{:S(2)}) %collective-permute-start.6) | collective-permute-done | bytes 98336 | tf_op jit(solution)/shard_map/ppermute | solution.py:234
  31.5 1.5 %collective-permute-done.8 = bf16[4,48,256]{2,1,0:T(8,128)(2,1)S(1)} collective-permute-done((bf16[4,48,256]{2,1,0:T(8,128)(2,1)S(1)}, bf16[4,48,256]{2,1,0:T(8,128)(2,1)S(1)}, u32[]{:S(2)}, u32[]{:S(2)}) %collective-permute-start.8) | collective-permute-done | bytes 98336 | tf_op jit(solution)/shard_map/ppermute | solution.py:234
  33.0 1.7 %collective-permute-done.7 = bf16[4,48,256]{2,1,0:T(8,128)(2,1)S(1)} collective-permute-done((bf16[4,48,256]{2,1,0:T(8,128)(2,1)S(1)}, bf16[4,48,256]{2,1,0:T(8,128)(2,1)S(1)}, u32[]{:S(2)}, u32[]{:S(2)}) %collective-permute-start.7) | collective-permute-done | bytes 98336 | tf_op jit(solution)/shard_map/ppermute | solution.py:234
  35.1 2.7 %collective-permute-start.10 = (bf16[4,48,256]{2,1,0:T(8,128)(2,1)S(1)}, bf16[4,48,256]{2,1,0:T(8,128)(2,1)S(1)}, u32[]{:S(2)}, u32[]{:S(2)}) collective-permute-start(bf16[4,48,256]{2,1,0:T(8,128)(2,1)S(1)} %pad_maximum_fusion.8), channel_id=1, source_target_pairs={{0,8},{1,9},{2,10},{3,11},{4,12},{5,13},{6,14},{7,15},{8,0},{9,1},... | collective-permute-start | bytes 294920 | tf_op jit(solution)/shard_map/ppermute | solution.py:234
  37.9 0.8 all-to-all-done.1
  39.1 2.8 %collective-permute-start.17 = (bf16[384,256]{1,0:T(8,128)(2,1)S(1)}, bf16[384,256]{1,0:T(8,128)(2,1)S(1)}, u32[]{:S(2)}, u32[]{:S(2)}) collective-permute-start(bf16[384,256]{1,0:T(8,128)(2,1)S(1)} %shard_map.84), channel_id=1, source_target_pairs={{0,3},{1,0},{2,1},{3,2},{4,7},{5,4},{6,5},{7,6},{8,11},{9,8},{10,9... | collective-permute-start | bytes 589832 | tf_op jit(solution)/shard_map/ppermute | solution.py:234
  42.2 1.4 %collective-permute-done.11 = bf16[4,48,256]{2,1,0:T(8,128)(2,1)S(1)} collective-permute-done((bf16[4,48,256]{2,1,0:T(8,128)(2,1)S(1)}, bf16[4,48,256]{2,1,0:T(8,128)(2,1)S(1)}, u32[]{:S(2)}, u32[]{:S(2)}) %collective-permute-start.11) | collective-permute-done | bytes 98336 | tf_op jit(solution)/shard_map/ppermute | solution.py:234
  43.7 0.8 shard_map.85
  45.2 0.8 collective-permute-start.12
  46.0 1.3 %collective-permute-start.13 = (bf16[256,384]{1,0:T(8,128)(2,1)S(1)}, bf16[256,384]{1,0:T(8,128)(2,1)S(1)}, u32[]{:S(2)}, u32[]{:S(2)}) collective-permute-start(bf16[256,384]{1,0:T(8,128)(2,1)S(1)} %get-tuple-element.62), channel_id=1, source_target_pairs={{0,12},{1,13},{2,14},{3,15},{4,0},{5,1},{6,2},{7,3},{8,4},{9,5},{1... | collective-permute-start | bytes 589832 | tf_op jit(solution)/shard_map/ppermute | solution.py:234
  47.4 3.3 %collective-permute-start.19 = (bf16[192,256]{1,0:T(8,128)(2,1)S(1)}, bf16[192,256]{1,0:T(8,128)(2,1)S(1)}, u32[]{:S(2)}, u32[]{:S(2)}) collective-permute-start(bf16[192,256]{1,0:T(8,128)(2,1)S(1)} %slice.237), channel_id=1, source_target_pairs={{0,3},{1,0},{2,1},{3,2},{4,7},{5,4},{6,5},{7,6},{8,11},{9,8},{10,9... | collective-permute-start | bytes 294920 | tf_op jit(solution)/shard_map/ppermute | solution.py:234
  51.4 1.6 %collective-permute-start.14 = (bf16[128,384]{1,0:T(8,128)(2,1)S(1)}, bf16[128,384]{1,0:T(8,128)(2,1)S(1)}, u32[]{:S(2)}, u32[]{:S(2)}) collective-permute-start(bf16[128,384]{1,0:T(8,128)(2,1)S(1)} %slice.234), channel_id=1, source_target_pairs={{0,4},{1,5},{2,6},{3,7},{4,8},{5,9},{6,10},{7,11},{8,12},{9,13},{1... | collective-permute-start | bytes 294920 | tf_op jit(solution)/shard_map/ppermute | solution.py:234
  53.6 3.4 %collective-permute-done.18 = bf16[192,256]{1,0:T(8,128)(2,1)S(1)} collective-permute-done((bf16[192,256]{1,0:T(8,128)(2,1)S(1)}, bf16[192,256]{1,0:T(8,128)(2,1)S(1)}, u32[]{:S(2)}, u32[]{:S(2)}) %collective-permute-start.18) | collective-permute-done | bytes 98336 | tf_op jit(solution)/shard_map/ppermute | solution.py:234
  57.2 1.8 %collective-permute-done.15 = bf16[128,384]{1,0:T(8,128)(2,1)S(1)} collective-permute-done((bf16[128,384]{1,0:T(8,128)(2,1)S(1)}, bf16[128,384]{1,0:T(8,128)(2,1)S(1)}, u32[]{:S(2)}, u32[]{:S(2)}) %collective-permute-start.15) | collective-permute-done | bytes 98336 | tf_op jit(solution)/shard_map/ppermute | solution.py:234
  59.2 3.2 %collective-permute-start.20 = (bf16[4,384,256]{2,1,0:T(8,128)(2,1)S(1)}, bf16[4,384,256]{2,1,0:T(8,128)(2,1)S(1)}, u32[]{:S(2)}, u32[]{:S(2)}) collective-permute-start(bf16[4,384,256]{2,1,0:T(8,128)(2,1)S(1)} %pad_maximum_fusion.5.refs_0_), channel_id=1, source_target_pairs={{0,4},{1,5},{2,6},{3,7},{4,8},{5,9},{6,10},{7,11},{8,12},{9,13},{1... | collective-permute-start | bytes 2359304 | tf_op jit(solution)/shard_map/ppermute | solution.py:234
  62.4 2.9 %collective-permute-start.25 = (bf16[4,256,384]{2,1,0:T(8,128)(2,1)S(1)}, bf16[4,256,384]{2,1,0:T(8,128)(2,1)S(1)}, u32[]{:S(2)}, u32[]{:S(2)}) collective-permute-start(bf16[4,256,384]{2,1,0:T(8,128)(2,1)S(1)} %pad_maximum_fusion.4.refs_5_), channel_id=1, source_target_pairs={{0,3},{1,0},{2,1},{3,2},{4,7},{5,4},{6,5},{7,6},{8,11},{9,8},{10,9... | collective-permute-start | bytes 2359304 | tf_op jit(solution)/shard_map/ppermute | solution.py:234
  65.4 12.0 %collective-permute-done.21.refs_2_ = bf16[4,384,256]{2,1,0:T(8,128)(2,1)S(1)} collective-permute-done((bf16[4,384,256]{2,1,0:T(8,128)(2,1)S(1)}, bf16[4,384,256]{2,1,0:T(8,128)(2,1)S(1)}, u32[]{:S(2)}, u32[]{:S(2)}) %collective-permute-start.21) | collective-permute-done | bytes 786464 | tf_op jit(solution)/shard_map/ppermute | solution.py:234
  77.5 3.3 %collective-permute-start.22 = (bf16[2,384,256]{2,1,0:T(8,128)(2,1)S(1)}, bf16[2,384,256]{2,1,0:T(8,128)(2,1)S(1)}, u32[]{:S(2)}, u32[]{:S(2)}) collective-permute-start(bf16[2,384,256]{2,1,0:T(8,128)(2,1)S(1)} %slice.238), channel_id=1, source_target_pairs={{0,4},{1,5},{2,6},{3,7},{4,8},{5,9},{6,10},{7,11},{8,12},{9,13},{1... | collective-permute-start | bytes 1179656 | tf_op jit(solution)/shard_map/ppermute | solution.py:234
  80.9 2.6 %collective-permute-start.27 = (bf16[2,256,384]{2,1,0:T(8,128)(2,1)S(1)}, bf16[2,256,384]{2,1,0:T(8,128)(2,1)S(1)}, u32[]{:S(2)}, u32[]{:S(2)}) collective-permute-start(bf16[2,256,384]{2,1,0:T(8,128)(2,1)S(1)} %slice.241), channel_id=1, source_target_pairs={{0,3},{1,0},{2,1},{3,2},{4,7},{5,4},{6,5},{7,6},{8,11},{9,8},{10,9... | collective-permute-start | bytes 1179656 | tf_op jit(solution)/shard_map/ppermute | solution.py:234
  83.6 2.8 %collective-permute-done.23.refs_4_ = bf16[2,384,256]{2,1,0:T(8,128)(2,1)S(1)} collective-permute-done((bf16[2,384,256]{2,1,0:T(8,128)(2,1)S(1)}, bf16[2,384,256]{2,1,0:T(8,128)(2,1)S(1)}, u32[]{:S(2)}, u32[]{:S(2)}) %collective-permute-start.23) | collective-permute-done | bytes 393248 | tf_op jit(solution)/shard_map/ppermute | solution.py:234
  86.5 2.3 %collective-permute-done.27.refs_9_ = bf16[2,256,384]{2,1,0:T(8,128)(2,1)S(1)} collective-permute-done((bf16[2,256,384]{2,1,0:T(8,128)(2,1)S(1)}, bf16[2,256,384]{2,1,0:T(8,128)(2,1)S(1)}, u32[]{:S(2)}, u32[]{:S(2)}) %collective-permute-start.27) | collective-permute-done | bytes 393248 | tf_op jit(solution)/shard_map/ppermute | solution.py:234
  88.8 3.8 %collective-permute-done.26.refs_8_ = bf16[2,256,384]{2,1,0:T(8,128)(2,1)S(1)} collective-permute-done((bf16[2,256,384]{2,1,0:T(8,128)(2,1)S(1)}, bf16[2,256,384]{2,1,0:T(8,128)(2,1)S(1)}, u32[]{:S(2)}, u32[]{:S(2)}) %collective-permute-start.26) | collective-permute-done | bytes 393248 | tf_op jit(solution)/shard_map/ppermute | solution.py:234
  92.6 12.5 %update.1 = f32[4096,256]{1,0:T(8,128)} custom-call(bf16[4,384,256]{2,1,0:T(8,128)(2,1)S(1)} %pad_maximum_fusion.5.refs_0_, bf16[4,384,256]{2,1,0:T(8,128)(2,1)S(1)} %collective-permute-done.20.refs_1_, bf16[4,384,256]{2,1,0:T(8,128)(2,1)S(1)} %collective-permute-done.21.refs_2_, bf16[2,384,256]{2,1,0:T(8,128)(2,1)S(1)} %collective-permute-done.22.refs_3_, ...), custom_call_target="tpu_custom_call" | custom-call | tf_op jit(solution)/shard_map/update/pallas_call | solution.py:422
  (52 shorter events, 4.0 us)
Async XLA Ops:
  0.0 19.0 %copy-start = (bf16[32,64,256]{2,1,0:T(8,128)(2,1)S(1)}, bf16[32,64,256]{2,1,0:T(8,128)(2,1)}, u32[]{:S(2)}) copy-start(bf16[32,64,256]{2,1,0:T(8,128)(2,1)} %param.11) | copy-start | bytes 3145732
  2.6 16.4 %all-to-all-start = ((f32[16,8,128]{2,1,0:T(8,128)}), f32[16,8,128]{2,1,0:T(8,128)S(1)}, u32[]{:S(2)}, u32[]{:S(2)}) async-start(f32[16,8,128]{2,1,0:T(8,128)} %bitcast.91), calls=%async_computation | async-start | bytes 131072 | tf_op jit(solution)/shard_map/all_to_all | solution.py:361
  11.2 27.5 %copy-start.1 = (bf16[6,1,64,256]{3,2,1,0:T(8,128)(2,1)S(1)}, bf16[6,1,64,256]{3,2,1,0:T(8,128)(2,1)}, u32[]{:S(2)}) copy-start(bf16[6,1,64,256]{3,2,1,0:T(8,128)(2,1)} %param.17) | copy-start | bytes 589828
  11.2 27.4 %copy-start.2 = (s32[384,128]{1,0:T(8,128)S(1)}, s32[384,128]{1,0:T(8,128)}, u32[]{:S(2)}) copy-start(s32[384,128]{1,0:T(8,128)} %get-tuple-element.56.target_ref) | copy-start | bytes 589828
  21.6 17.1 %all-to-all-start.1 = ((bf16[16,48,256]{2,1,0:T(8,128)(2,1)}), bf16[16,48,256]{2,1,0:T(8,128)(2,1)S(1)}, u32[]{:S(2)}, u32[]{:S(2)}) async-start(bf16[16,48,256]{2,1,0:T(8,128)(2,1)} %get-tuple-element.54), calls=%async_computation.1 | async-start | bytes 786432 | tf_op jit(solution)/shard_map/all_to_all | solution.py:402
  25.2 6.3 %collective-permute-start.6 = (bf16[4,48,256]{2,1,0:T(8,128)(2,1)S(1)}, bf16[4,48,256]{2,1,0:T(8,128)(2,1)S(1)}, u32[]{:S(2)}, u32[]{:S(2)}) collective-permute-start(bf16[4,48,256]{2,1,0:T(8,128)(2,1)S(1)} %get-tuple-element.100), channel_id=1, source_target_pairs={{0,1},{1,2},{2,3},{3,0},{4,5},{5,6},{6,7},{7,4},{8,9},{9,10},{10,1... | collective-permute-start | bytes 294920 | tf_op jit(solution)/shard_map/ppermute | solution.py:234
  26.8 6.2 %collective-permute-start.8 = (bf16[4,48,256]{2,1,0:T(8,128)(2,1)S(1)}, bf16[4,48,256]{2,1,0:T(8,128)(2,1)S(1)}, u32[]{:S(2)}, u32[]{:S(2)}) collective-permute-start(bf16[4,48,256]{2,1,0:T(8,128)(2,1)S(1)} %get-tuple-element.101), channel_id=1, source_target_pairs={{0,3},{1,0},{2,1},{3,2},{4,7},{5,4},{6,5},{7,6},{8,11},{9,8},{10,9... | collective-permute-start | bytes 294920 | tf_op jit(solution)/shard_map/ppermute | solution.py:234
  28.6 6.1 %collective-permute-start.7 = (bf16[4,48,256]{2,1,0:T(8,128)(2,1)S(1)}, bf16[4,48,256]{2,1,0:T(8,128)(2,1)S(1)}, u32[]{:S(2)}, u32[]{:S(2)}) collective-permute-start(bf16[4,48,256]{2,1,0:T(8,128)(2,1)S(1)} %get-tuple-element.102), channel_id=1, source_target_pairs={{0,2},{1,3},{2,0},{3,1},{4,6},{5,7},{6,4},{7,5},{8,10},{9,11},{10,... | collective-permute-start | bytes 294920 | tf_op jit(solution)/shard_map/ppermute | solution.py:234
  34.7 7.2 %collective-permute-start.9 = (bf16[4,48,256]{2,1,0:T(8,128)(2,1)S(1)}, bf16[4,48,256]{2,1,0:T(8,128)(2,1)S(1)}, u32[]{:S(2)}, u32[]{:S(2)}) collective-permute-start(bf16[4,48,256]{2,1,0:T(8,128)(2,1)S(1)} %pad_maximum_fusion.7), channel_id=1, source_target_pairs={{0,4},{1,5},{2,6},{3,7},{4,8},{5,9},{6,10},{7,11},{8,12},{9,13},{1... | collective-permute-start | bytes 294920 | tf_op jit(solution)/shard_map/ppermute | solution.py:234
  35.1 7.1 %collective-permute-start.10 = (bf16[4,48,256]{2,1,0:T(8,128)(2,1)S(1)}, bf16[4,48,256]{2,1,0:T(8,128)(2,1)S(1)}, u32[]{:S(2)}, u32[]{:S(2)}) collective-permute-start(bf16[4,48,256]{2,1,0:T(8,128)(2,1)S(1)} %pad_maximum_fusion.8), channel_id=1, source_target_pairs={{0,8},{1,9},{2,10},{3,11},{4,12},{5,13},{6,14},{7,15},{8,0},{9,1},... | collective-permute-start | bytes 294920 | tf_op jit(solution)/shard_map/ppermute | solution.py:234
  37.8 5.9 %collective-permute-start.11 = (bf16[4,48,256]{2,1,0:T(8,128)(2,1)S(1)}, bf16[4,48,256]{2,1,0:T(8,128)(2,1)S(1)}, u32[]{:S(2)}, u32[]{:S(2)}) collective-permute-start(bf16[4,48,256]{2,1,0:T(8,128)(2,1)S(1)} %pad_maximum_fusion.9), channel_id=1, source_target_pairs={{0,12},{1,13},{2,14},{3,15},{4,0},{5,1},{6,2},{7,3},{8,4},{9,5},{1... | collective-permute-start | bytes 294920 | tf_op jit(solution)/shard_map/ppermute | solution.py:234
  39.1 8.3 %collective-permute-start.17 = (bf16[384,256]{1,0:T(8,128)(2,1)S(1)}, bf16[384,256]{1,0:T(8,128)(2,1)S(1)}, u32[]{:S(2)}, u32[]{:S(2)}) collective-permute-start(bf16[384,256]{1,0:T(8,128)(2,1)S(1)} %shard_map.84), channel_id=1, source_target_pairs={{0,3},{1,0},{2,1},{3,2},{4,7},{5,4},{6,5},{7,6},{8,11},{9,8},{10,9... | collective-permute-start | bytes 589832 | tf_op jit(solution)/shard_map/ppermute | solution.py:234
  41.9 8.9 %collective-permute-start.16 = (bf16[384,256]{1,0:T(8,128)(2,1)S(1)}, bf16[384,256]{1,0:T(8,128)(2,1)S(1)}, u32[]{:S(2)}, u32[]{:S(2)}) collective-permute-start(bf16[384,256]{1,0:T(8,128)(2,1)S(1)} %shard_map.84), channel_id=1, source_target_pairs={{0,1},{1,2},{2,3},{3,0},{4,5},{5,6},{6,7},{7,4},{8,9},{9,10},{10,1... | collective-permute-start | bytes 589832 | tf_op jit(solution)/shard_map/ppermute | solution.py:234
  45.2 47.4 %copy-start.3 = (f32[4096,256]{1,0:T(8,128)S(1)}, f32[4096,256]{1,0:T(8,128)}, u32[]{:S(2)}) copy-start(f32[4096,256]{1,0:T(8,128)} %get-tuple-element.234) | copy-start | bytes 12582916
  45.2 6.2 %collective-permute-start.12 = (bf16[256,384]{1,0:T(8,128)(2,1)S(1)}, bf16[256,384]{1,0:T(8,128)(2,1)S(1)}, u32[]{:S(2)}, u32[]{:S(2)}) collective-permute-start(bf16[256,384]{1,0:T(8,128)(2,1)S(1)} %get-tuple-element.62), channel_id=1, source_target_pairs={{0,4},{1,5},{2,6},{3,7},{4,8},{5,9},{6,10},{7,11},{8,12},{9,13},{1... | collective-permute-start | bytes 589832 | tf_op jit(solution)/shard_map/ppermute | solution.py:234
  46.0 7.0 %collective-permute-start.13 = (bf16[256,384]{1,0:T(8,128)(2,1)S(1)}, bf16[256,384]{1,0:T(8,128)(2,1)S(1)}, u32[]{:S(2)}, u32[]{:S(2)}) collective-permute-start(bf16[256,384]{1,0:T(8,128)(2,1)S(1)} %get-tuple-element.62), channel_id=1, source_target_pairs={{0,12},{1,13},{2,14},{3,15},{4,0},{5,1},{6,2},{7,3},{8,4},{9,5},{1... | collective-permute-start | bytes 589832 | tf_op jit(solution)/shard_map/ppermute | solution.py:234
  47.4 6.3 %collective-permute-start.19 = (bf16[192,256]{1,0:T(8,128)(2,1)S(1)}, bf16[192,256]{1,0:T(8,128)(2,1)S(1)}, u32[]{:S(2)}, u32[]{:S(2)}) collective-permute-start(bf16[192,256]{1,0:T(8,128)(2,1)S(1)} %slice.237), channel_id=1, source_target_pairs={{0,3},{1,0},{2,1},{3,2},{4,7},{5,4},{6,5},{7,6},{8,11},{9,8},{10,9... | collective-permute-start | bytes 294920 | tf_op jit(solution)/shard_map/ppermute | solution.py:234
  50.9 6.2 %collective-permute-start.18 = (bf16[192,256]{1,0:T(8,128)(2,1)S(1)}, bf16[192,256]{1,0:T(8,128)(2,1)S(1)}, u32[]{:S(2)}, u32[]{:S(2)}) collective-permute-start(bf16[192,256]{1,0:T(8,128)(2,1)S(1)} %slice.236), channel_id=1, source_target_pairs={{0,1},{1,2},{2,3},{3,0},{4,5},{5,6},{6,7},{7,4},{8,9},{9,10},{10,1... | collective-permute-start | bytes 294920 | tf_op jit(solution)/shard_map/ppermute | solution.py:234
  51.4 5.7 %collective-permute-start.14 = (bf16[128,384]{1,0:T(8,128)(2,1)S(1)}, bf16[128,384]{1,0:T(8,128)(2,1)S(1)}, u32[]{:S(2)}, u32[]{:S(2)}) collective-permute-start(bf16[128,384]{1,0:T(8,128)(2,1)S(1)} %slice.234), channel_id=1, source_target_pairs={{0,4},{1,5},{2,6},{3,7},{4,8},{5,9},{6,10},{7,11},{8,12},{9,13},{1... | collective-permute-start | bytes 294920 | tf_op jit(solution)/shard_map/ppermute | solution.py:234
  53.0 5.9 %collective-permute-start.15 = (bf16[128,384]{1,0:T(8,128)(2,1)S(1)}, bf16[128,384]{1,0:T(8,128)(2,1)S(1)}, u32[]{:S(2)}, u32[]{:S(2)}) collective-permute-start(bf16[128,384]{1,0:T(8,128)(2,1)S(1)} %slice.235), channel_id=1, source_target_pairs={{0,12},{1,13},{2,14},{3,15},{4,0},{5,1},{6,2},{7,3},{8,4},{9,5},{1... | collective-permute-start | bytes 294920 | tf_op jit(solution)/shard_map/ppermute | solution.py:234
  59.1 18.3 %collective-permute-start.21 = (bf16[4,384,256]{2,1,0:T(8,128)(2,1)S(1)}, bf16[4,384,256]{2,1,0:T(8,128)(2,1)S(1)}, u32[]{:S(2)}, u32[]{:S(2)}) collective-permute-start(bf16[4,384,256]{2,1,0:T(8,128)(2,1)S(1)} %pad_maximum_fusion.5.refs_0_), channel_id=1, source_target_pairs={{0,12},{1,13},{2,14},{3,15},{4,0},{5,1},{6,2},{7,3},{8,4},{9,5},{1... | collective-permute-start | bytes 2359304 | tf_op jit(solution)/shard_map/ppermute | solution.py:234
  59.2 18.3 %collective-permute-start.20 = (bf16[4,384,256]{2,1,0:T(8,128)(2,1)S(1)}, bf16[4,384,256]{2,1,0:T(8,128)(2,1)S(1)}, u32[]{:S(2)}, u32[]{:S(2)}) collective-permute-start(bf16[4,384,256]{2,1,0:T(8,128)(2,1)S(1)} %pad_maximum_fusion.5.refs_0_), channel_id=1, source_target_pairs={{0,4},{1,5},{2,6},{3,7},{4,8},{5,9},{6,10},{7,11},{8,12},{9,13},{1... | collective-permute-start | bytes 2359304 | tf_op jit(solution)/shard_map/ppermute | solution.py:234
  62.4 18.4 %collective-permute-start.25 = (bf16[4,256,384]{2,1,0:T(8,128)(2,1)S(1)}, bf16[4,256,384]{2,1,0:T(8,128)(2,1)S(1)}, u32[]{:S(2)}, u32[]{:S(2)}) collective-permute-start(bf16[4,256,384]{2,1,0:T(8,128)(2,1)S(1)} %pad_maximum_fusion.4.refs_5_), channel_id=1, source_target_pairs={{0,3},{1,0},{2,1},{3,2},{4,7},{5,4},{6,5},{7,6},{8,11},{9,8},{10,9... | collective-permute-start | bytes 2359304 | tf_op jit(solution)/shard_map/ppermute | solution.py:234
  65.4 18.1 %collective-permute-start.24 = (bf16[4,256,384]{2,1,0:T(8,128)(2,1)S(1)}, bf16[4,256,384]{2,1,0:T(8,128)(2,1)S(1)}, u32[]{:S(2)}, u32[]{:S(2)}) collective-permute-start(bf16[4,256,384]{2,1,0:T(8,128)(2,1)S(1)} %pad_maximum_fusion.4.refs_5_), channel_id=1, source_target_pairs={{0,1},{1,2},{2,3},{3,0},{4,5},{5,6},{6,7},{7,4},{8,9},{9,10},{10,1... | collective-permute-start | bytes 2359304 | tf_op jit(solution)/shard_map/ppermute | solution.py:234
  77.4 9.1 %collective-permute-start.23 = (bf16[2,384,256]{2,1,0:T(8,128)(2,1)S(1)}, bf16[2,384,256]{2,1,0:T(8,128)(2,1)S(1)}, u32[]{:S(2)}, u32[]{:S(2)}) collective-permute-start(bf16[2,384,256]{2,1,0:T(8,128)(2,1)S(1)} %slice.239), channel_id=1, source_target_pairs={{0,12},{1,13},{2,14},{3,15},{4,0},{5,1},{6,2},{7,3},{8,4},{9,5},{1... | collective-permute-start | bytes 1179656 | tf_op jit(solution)/shard_map/ppermute | solution.py:234
  77.5 8.9 %collective-permute-start.22 = (bf16[2,384,256]{2,1,0:T(8,128)(2,1)S(1)}, bf16[2,384,256]{2,1,0:T(8,128)(2,1)S(1)}, u32[]{:S(2)}, u32[]{:S(2)}) collective-permute-start(bf16[2,384,256]{2,1,0:T(8,128)(2,1)S(1)} %slice.238), channel_id=1, source_target_pairs={{0,4},{1,5},{2,6},{3,7},{4,8},{5,9},{6,10},{7,11},{8,12},{9,13},{1... | collective-permute-start | bytes 1179656 | tf_op jit(solution)/shard_map/ppermute | solution.py:234
  80.9 7.9 %collective-permute-start.27 = (bf16[2,256,384]{2,1,0:T(8,128)(2,1)S(1)}, bf16[2,256,384]{2,1,0:T(8,128)(2,1)S(1)}, u32[]{:S(2)}, u32[]{:S(2)}) collective-permute-start(bf16[2,256,384]{2,1,0:T(8,128)(2,1)S(1)} %slice.241), channel_id=1, source_target_pairs={{0,3},{1,0},{2,1},{3,2},{4,7},{5,4},{6,5},{7,6},{8,11},{9,8},{10,9... | collective-permute-start | bytes 1179656 | tf_op jit(solution)/shard_map/ppermute | solution.py:234
  83.5 9.1 %collective-permute-start.26 = (bf16[2,256,384]{2,1,0:T(8,128)(2,1)S(1)}, bf16[2,256,384]{2,1,0:T(8,128)(2,1)S(1)}, u32[]{:S(2)}, u32[]{:S(2)}) collective-permute-start(bf16[2,256,384]{2,1,0:T(8,128)(2,1)S(1)} %slice.240), channel_id=1, source_target_pairs={{0,1},{1,2},{2,3},{3,0},{4,5},{5,6},{6,7},{7,4},{8,9},{9,10},{10,1... | collective-permute-start | bytes 1179656 | tf_op jit(solution)/shard_map/ppermute | solution.py:234
